TPU v7x, 512 devices: a whole 4x4x16 slice. The times are simulated.
512 devices in a mesh: orbit: 8 (over x, core), lon: 64 (over y, z).
Axes of the slice: x: 4, y: 4, z: 16, core: 2. Of those that a mesh axis runs over, the one named last changes fastest.
Arguments:
- interp: bfloat16 [256, 64, 256, 128], P('orbit', 'lon'), may hold values from -0.5 to 0.5
- obs_value: float32 [256, 64, 256], P('orbit', 'lon'), may hold values from -20 to 20
- obs_weight: float32 [256, 64, 256], P('orbit', 'lon'), may hold values from 0.5 to 4
- block_map: int32 [256, 64], P('orbit', 'lon'), may hold values from 0 to 511
- live_count: int32 [8, 64], P('orbit', 'lon'), may hold values from 4 to 32, as said below
- kappa2: float32 [4096, 1024], P('lon'), may hold values from 0.01 to 1
Outputs:
- solution: float32 [4096, 1024], P('lon')
- residual: float32 [4096, 1024], P('lon')
Inputs may be any that keep to these rules, and one draw needn't show every extreme that they name: `live_count`: live blocks of the device of orbit group o in band l; its slots at or beyond this count are padding; some device holds exactly 32.
All inputs are finite; a program needn't handle non-finite values.
Results may differ from a plain program's by a relative error of at most 0.014.
Values sent between devices are 32-bit elements; how exact they have to be, the bound alone decides.
A program may use at most 64 MiB of HBM per device.

v0:
```python
import math

import jax
import jax.numpy as jnp
from jax import lax
from jax.sharding import PartitionSpec as P

ITERS = 2


prior_weight = 0.0625


def with_halo(cells, sides, width):
    for axis, dim in sides:
        count = lax.axis_size(axis)
        head = lax.slice_in_dim(cells, 0, width, axis=dim)
        tail = lax.slice_in_dim(cells, cells.shape[dim] - width, cells.shape[dim], axis=dim)
        cells = jnp.concatenate(
            [
                lax.ppermute(tail, axis, [(i, (i + 1) % count) for i in range(count)]),
                cells,
                lax.ppermute(head, axis, [((i + 1) % count, i) for i in range(count)]),
            ],
            axis=dim,
        )
    return cells


def lat_pair(field):
    padded = jnp.pad(field, ((0, 0), (1, 1)))
    return padded[:, 2:] + padded[:, :-2]


def stencil(extended, kappa_rows):
    center = extended[1:-1]
    return (kappa_rows + 4.0) * center - extended[2:] - extended[:-2] - lat_pair(center)


def thin_rim(field):
    return with_halo(field, (("lon", 0),), 1)


def prior_term(field, kappa2):
    first = stencil(thin_rim(field), kappa2)
    return prior_weight * stencil(thin_rim(first), kappa2)


def scatter_blocks(terms, targets, block_total):
    return jnp.zeros((block_total, terms.shape[1]), jnp.float32).at[targets].add(terms)


def slot_terms(field, matrices, weights, targets, live, count):
    cell_width = matrices.shape[2]
    cell_rows = field.astype(jnp.bfloat16).reshape(-1, cell_width)
    slot_total = matrices.shape[0]
    group_width = math.gcd(slot_total, 8)
    passes = (count + group_width - 1) // group_width

    def advance(turn, gathered):
        offset = turn * group_width
        block = lax.dynamic_slice_in_dim(matrices, offset, group_width, 0)
        weight_part = lax.dynamic_slice_in_dim(weights, offset, group_width, 0)
        target_part = lax.dynamic_slice_in_dim(targets, offset, group_width, 0)
        live_part = lax.dynamic_slice_in_dim(live, offset, group_width, 0)
        picked = cell_rows[target_part]
        predicted = jnp.einsum("sqc,sc->sq", block, picked, preferred_element_type=jnp.float32)
        scaled = (weight_part * predicted).astype(jnp.bfloat16)
        back = (
            jnp.einsum("sqc,sq->sc", block, scaled, preferred_element_type=jnp.float32)
            * live_part[:, None]
        )
        return lax.dynamic_update_slice_in_dim(gathered, back, offset, 0)

    return lax.fori_loop(0, passes, advance, jnp.zeros((slot_total, cell_width), jnp.float32))


def residual_product(value):
    return lax.psum(value, "lon")


def per_device(interp, obs_value, obs_weight, block_map, live_count, kappa2):
    matrices = interp[:, 0]
    values = obs_value[:, 0]
    weights = obs_weight[:, 0]
    targets = block_map[:, 0]
    count = live_count[0, 0]
    slot_total = matrices.shape[0]
    live = (jnp.arange(slot_total) < count).astype(jnp.float32)
    block_total = kappa2.size // matrices.shape[2]
    field_shape = kappa2.shape
    scaled_data = (weights * values).astype(jnp.bfloat16)
    data_slots = (
        jnp.einsum("sqc,sq->sc", matrices, scaled_data, preferred_element_type=jnp.float32)
        * live[:, None]
    )
    squared = jnp.square(matrices.astype(jnp.float32))
    diagonal_slots = (
        jnp.einsum("sqc,sq->sc", squared, weights, precision=lax.Precision.HIGHEST) * live[:, None]
    )
    right_side, obs_diag = lax.psum(
        (
            scatter_blocks(data_slots, targets, block_total),
            scatter_blocks(diagonal_slots, targets, block_total),
        ),
        "orbit",
    )
    right_side = right_side.reshape(field_shape)
    obs_diag = obs_diag.reshape(field_shape)
    precond = prior_weight * ((kappa2 + 4.0) ** 2 + 4.0) + obs_diag
    solution = jnp.zeros_like(right_side)
    residual = right_side
    scaled_res = residual / precond
    direction = scaled_res
    product_now = residual_product(jnp.sum(residual * scaled_res))
    for turn in range(ITERS):
        terms = slot_terms(direction, matrices, weights, targets, live, count)
        normal = lax.psum(scatter_blocks(terms, targets, block_total), "orbit")
        image = prior_term(direction, kappa2) + normal.reshape(field_shape)
        alpha = product_now / lax.psum(jnp.sum(direction * image), "lon")
        solution = solution + alpha * direction
        residual = residual - alpha * image
        if turn + 1 < ITERS:
            scaled_res = residual / precond
            product_next = residual_product(jnp.sum(residual * scaled_res))
            direction = scaled_res + product_next / product_now * direction
            product_now = product_next
    return (solution, residual)


def solution(mesh):
    in_specs = (
        P("orbit", "lon", None, None),
        P("orbit", "lon", None),
        P("orbit", "lon", None),
        P("orbit", "lon"),
        P("orbit", "lon"),
        P("lon", None),
    )
    out_specs = (P("lon", None), P("lon", None))
    return jax.shard_map(
        per_device, mesh=mesh, in_specs=in_specs, out_specs=out_specs, check_vma=False
    )
```

profile of v0, /device:TPU:2, one launch (start us, length us, event | category | flops | bytes accessed | tf_op | source)
XLA Modules:
  0.0 710.5 jit_solution(2677517351619971608)
XLA Ops:
  7.2 0.0 copy-start
  7.2 0.0 all-reduce.14.cloned.1.call-start
  8.0 0.7 fusion.62
  8.7 0.8 fusion.57
  9.5 4.1 fusion.20
  13.6 0.0 copy-start.5
  13.6 0.4 fusion.55
  14.0 0.8 scatter_custom_fusion
  14.8 0.7 reshape.29
  15.6 0.8 scatter_custom_fusion.1
  16.4 0.7 reshape.30
  17.2 0.0 all-reduce.14.cloned.1.call-update
  17.2 0.0 all-reduce.10.cloned.1.call-start
  17.3 78.8 %all-reduce.14.cloned.1.call-done = (f32[64,1024]{1,0:T(8,128)}, f32[64,1024]{1,0:T(8,128)}) async-done(((f32[64,1024]{1,0:T(8,128)}, f32[64,1024]{1,0:T(8,128)}), (f32[64,1024]{1,0:T(8,128)}, f32[64,1024]{1,0:T(8,128)})) %all-reduce.14.cloned.1.call-update) | async-done | bytes 524304 | tf_op jit(solution)/shard_map/psum | solution.py:101
  96.1 1.1 fusion.68
  97.2 0.1 reshape.31
  97.3 8.1 %collective-permute-start = (f32[1,1024]{1,0:T(1,128)S(1)}, f32[1,1024]{1,0:T(1,128)S(1)}, u32[]{:S(2)}, u32[]{:S(2)}) collective-permute-start(f32[1,1024]{1,0:T(1,128)S(1)} %get-tuple-element.143), channel_id=1, source_target_pairs={{1,0},{2,1},{3,2},{4,3},{5,4},{6,5},{7,6},{8,7},{9,8},{10,9},{11,1... | collective-permute-start | bytes 12296 | tf_op jit(solution)/shard_map/ppermute | solution.py:23
  105.5 1.9 collective-permute-start.1
  107.4 1.3 while.20
  107.4 0.1 compare_select_fusion.5
  107.5 0.6 gather_fusion
  108.1 0.2 fusion.92
  108.3 0.2 fusion.94
  108.5 0.1 dynamic_slice.54
  108.6 0.1 multiply_dynamic-update-slice_fusion.4
  108.7 0.6 copy-done.4
  109.3 0.8 scatter_custom_fusion.2
  110.1 0.7 reshape.32
  110.8 0.0 all-reduce.10.cloned.1.call-update
  110.9 0.0 all-reduce.12.cloned.1.call-start
  110.9 3.4 collective-permute-done.1
  114.3 0.2 fusion.24
  114.5 3.9 collective-permute-start.2
  118.4 1.9 collective-permute-start.3
  120.4 6.9 collective-permute-done.3
  127.2 57.6 %all-reduce.10.cloned.1.call-done = f32[64,1024]{1,0:T(8,128)} async-done(((f32[64,1024]{1,0:T(8,128)}), f32[64,1024]{1,0:T(8,128)}) %all-reduce.10.cloned.1.call-update) | async-done | bytes 262160 | tf_op jit(solution)/shard_map/psum | solution.py:118
  184.9 2.5 multiply_reduce_fusion.2
  187.4 144.7 %all-reduce.4 = (f32[]{:T(128)}, f32[]{:T(128)}) all-reduce(f32[]{:T(128)} %get-tuple-element.91, f32[]{:T(128)} %get-tuple-element.90), channel_id=1, replica_groups=mesh['orbit'=8,'lon'=64] {'lon'}, use_global_device_ids=true, to_apply=%region_5.0 | all-reduce | flops 2 | bytes 16 | tf_op jit(solution)/shard_map/psum | solution.py:79
  333.5 1.7 multiply_reduce_fusion.1
  335.2 138.5 %psum.61 = f32[]{:T(128)} all-reduce(f32[]{:T(128)} %get-tuple-element.132), channel_id=1, replica_groups=mesh['orbit'=8,'lon'=64] {'lon'}, use_global_device_ids=true, to_apply=%region_13.14 | all-reduce | flops 1 | bytes 8 | tf_op jit(solution)/shard_map/psum | solution.py:79
  475.0 0.1 fusion.66
  475.2 3.9 collective-permute-start.4
  479.1 1.9 collective-permute-start.5
  481.0 0.1 reshape.33
  481.1 2.0 while.21
  481.1 0.1 compare_select_fusion.6
  481.2 0.6 gather_fusion.1
  481.8 0.2 fusion.99
  482.0 0.7 fusion.100
  482.7 0.2 fusion.101
  482.9 0.1 dynamic_slice.59
  483.0 0.1 multiply_dynamic-update-slice_fusion.5
  483.1 0.8 scatter_custom_fusion.3
  483.9 0.7 reshape.34
  484.6 0.0 all-reduce.12.cloned.1.call-update
  484.6 3.3 collective-permute-done.5
  487.9 0.2 fusion.30
  488.1 4.0 collective-permute-start.6
  492.1 1.9 collective-permute-start.7
  494.1 6.9 collective-permute-done.7
  500.9 54.3 %all-reduce.12.cloned.1.call-done = f32[64,1024]{1,0:T(8,128)} async-done(((f32[64,1024]{1,0:T(8,128)}), f32[64,1024]{1,0:T(8,128)}) %all-reduce.12.cloned.1.call-update) | async-done | bytes 262160 | tf_op jit(solution)/shard_map/psum | solution.py:118
  555.3 1.8 multiply_reduce_fusion
  557.0 144.8 %psum.63 = f32[]{:T(128)} all-reduce(f32[]{:T(128)} %get-tuple-element.128), channel_id=1, replica_groups=mesh['orbit'=8,'lon'=64] {'lon'}, use_global_device_ids=true, to_apply=%region_19.20 | all-reduce | flops 1 | bytes 8 | tf_op jit(solution)/shard_map/psum | solution.py:120
  703.1 0.9 multiply_subtract_fusion
  (26 shorter events, 0.1 us)
Async XLA Ops:
  7.2 6.4 copy-start
  7.2 88.9 %all-reduce.14.cloned.1.call-start = ((), (), s32[]{:S(2)}) async-start(), calls=%async_computation.2 | async-start | bytes 1048576 | tf_op jit(solution)/shard_map/psum | solution.py:101
  13.6 3.7 copy-start.5
  13.6 82.5 %copy-start.1 = (f32[64,1024]{1,0:T(8,128)S(1)}, f32[64,1024]{1,0:T(8,128)}, u32[]{:S(2)}) copy-start(f32[64,1024]{1,0:T(8,128)} %param.15) | copy-start | bytes 786436
  14.0 93.4 %copy-start.6 = (s32[32,1]{0,1:T(1,128)S(1)}, s32[32,1]{0,1:T(1,128)}, u32[]{:S(2)}) copy-start(s32[32,1]{0,1:T(1,128)} %param.13) | copy-start | bytes 388
  17.2 167.7 %all-reduce.10.cloned.1.call-start = ((), (), s32[]{:S(2)}) async-start(), calls=%async_computation | async-start | bytes 524288 | tf_op jit(solution)/shard_map/psum | solution.py:118
  97.3 13.6 %collective-permute-start = (f32[1,1024]{1,0:T(1,128)S(1)}, f32[1,1024]{1,0:T(1,128)S(1)}, u32[]{:S(2)}, u32[]{:S(2)}) collective-permute-start(f32[1,1024]{1,0:T(1,128)S(1)} %get-tuple-element.143), channel_id=1, source_target_pairs={{1,0},{2,1},{3,2},{4,3},{5,4},{6,5},{7,6},{8,7},{9,8},{10,9},{11,1... | collective-permute-start | bytes 12296 | tf_op jit(solution)/shard_map/ppermute | solution.py:23
  105.5 8.8 %collective-permute-start.1 = (f32[1,1024]{1,0:T(1,128)S(1)}, f32[1,1024]{1,0:T(1,128)S(1)}, u32[]{:S(2)}, u32[]{:S(2)}) collective-permute-start(f32[1,1024]{1,0:T(1,128)S(1)} %get-tuple-element.144), channel_id=1, source_target_pairs={{0,1},{1,2},{2,3},{3,4},{4,5},{5,6},{6,7},{7,8},{8,9},{9,10},{10,1... | collective-permute-start | bytes 12296 | tf_op jit(solution)/shard_map/ppermute | solution.py:21
  107.4 77.5 %copy-start.3 = (f32[64,1024]{1,0:T(8,128)S(1)}, f32[64,1024]{1,0:T(8,128)}, u32[]{:S(2)}) copy-start(f32[64,1024]{1,0:T(8,128)} %get-tuple-element.126) | copy-start | bytes 786436
  108.7 0.6 copy-start.4
  109.3 224.2 %copy-start.2 = (f32[64,1024]{1,0:T(8,128)S(1)}, f32[64,1024]{1,0:T(8,128)}, u32[]{:S(2)}) copy-start(f32[64,1024]{1,0:T(8,128)} %get-tuple-element.127) | copy-start | bytes 786436
  110.9 444.4 %all-reduce.12.cloned.1.call-start = ((), (), s32[]{:S(2)}) async-start(), calls=%async_computation.1 | async-start | bytes 524288 | tf_op jit(solution)/shard_map/psum | solution.py:118
  114.5 5.9 collective-permute-start.2
  118.4 8.8 %collective-permute-start.3 = (f32[1,1024]{1,0:T(1,128)S(1)}, f32[1,1024]{1,0:T(1,128)S(1)}, u32[]{:S(2)}, u32[]{:S(2)}) collective-permute-start(f32[1,1024]{1,0:T(1,128)S(1)} %get-tuple-element.142), channel_id=1, source_target_pairs={{0,1},{1,2},{2,3},{3,4},{4,5},{5,6},{6,7},{7,8},{8,9},{9,10},{10,1... | collective-permute-start | bytes 12296 | tf_op jit(solution)/shard_map/ppermute | solution.py:21
  475.2 9.5 %collective-permute-start.4 = (f32[1,1024]{1,0:T(1,128)S(1)}, f32[1,1024]{1,0:T(1,128)S(1)}, u32[]{:S(2)}, u32[]{:S(2)}) collective-permute-start(f32[1,1024]{1,0:T(1,128)S(1)} %get-tuple-element.139), channel_id=1, source_target_pairs={{1,0},{2,1},{3,2},{4,3},{5,4},{6,5},{7,6},{8,7},{9,8},{10,9},{11,1... | collective-permute-start | bytes 12296 | tf_op jit(solution)/shard_map/ppermute | solution.py:23
  479.1 8.8 %collective-permute-start.5 = (f32[1,1024]{1,0:T(1,128)S(1)}, f32[1,1024]{1,0:T(1,128)S(1)}, u32[]{:S(2)}, u32[]{:S(2)}) collective-permute-start(f32[1,1024]{1,0:T(1,128)S(1)} %get-tuple-element.140), channel_id=1, source_target_pairs={{0,1},{1,2},{2,3},{3,4},{4,5},{5,6},{6,7},{7,8},{8,9},{9,10},{10,1... | collective-permute-start | bytes 12296 | tf_op jit(solution)/shard_map/ppermute | solution.py:21
  488.1 5.9 collective-permute-start.6
  492.1 8.8 %collective-permute-start.7 = (f32[1,1024]{1,0:T(1,128)S(1)}, f32[1,1024]{1,0:T(1,128)S(1)}, u32[]{:S(2)}, u32[]{:S(2)}) collective-permute-start(f32[1,1024]{1,0:T(1,128)S(1)} %get-tuple-element.138), channel_id=1, source_target_pairs={{0,1},{1,2},{2,3},{3,4},{4,5},{5,6},{6,7},{7,8},{8,9},{9,10},{10,1... | collective-permute-start | bytes 12296 | tf_op jit(solution)/shard_map/ppermute | solution.py:21
Sparse Core Ops, SparseCore 0:
  17.3 78.7 all-reduce.13
  111.0 73.8 all-reduce.9
  484.7 70.4 all-reduce.11
where the time goes:
time: 711 us
  blocking collectives  428 us (60%)
  waiting for transfers between devices  211 us (30%)
  starting transfers between devices  27.8 us (4%)
  between operations  18.8 us (3%)
  other arithmetic  14.2 us (2%)
    psum x2, blocking collectives, residual_product(): return lax.psum(value, 'lon')  283 us
    psum x1, blocking collectives, per_device(): alpha = product_now / lax.psum(jnp.sum(direction * image), 'lon')  145 us
    psum x2, waiting for transfers between devices, per_device(): normal = lax.psum(scatter_blocks(terms, targets, block_total), 'orbit')  112 us
    psum x1, waiting for transfers between devices, per_device(): lax.psum((scatter_blocks(data_slots, targets, block_total), scatter_block...  78.8 us
    ppermute x4, waiting for transfers between devices, with_halo(): lax.ppermute(tail, axis, [(i, (i + 1) % count) for i in range(count)])  20.4 us
    ppermute x4, starting transfers between devices, with_halo(): lax.ppermute(head, axis, [((i + 1) % count, i) for i in range(count)])  19.9 us
  transfers between devices with their start and end apart: 11, of which 7 were waited for; matrix products, arithmetic and copies ran while one was open for 1% of the time, Pallas kernels for 0%

commit v1 on v0

v1 whole, which is shorter than its diff:
```python
import functools

import jax
import jax.numpy as jnp
from jax import lax
from jax.experimental import pallas as pl
from jax.experimental.pallas import tpu as pltpu
from jax.sharding import PartitionSpec as P

MESH = pl.DeviceIdType.MESH
F32 = jnp.float32
BF16 = jnp.bfloat16

prior_weight = 0.0625
SUB = 8
CHUNKS = 4


def split(value):
    high = value.astype(BF16)
    return high, (value - high.astype(F32)).astype(BF16)


def lat_pair(cells, lane, sub):
    up = pltpu.roll(cells, 127, axis=2)
    down = pltpu.roll(cells, 1, axis=2)
    up_edge = jnp.where(sub == SUB - 1, 0.0, pltpu.roll(up, SUB - 1, axis=1))
    down_edge = jnp.where(sub == 0, 0.0, pltpu.roll(down, 1, axis=1))
    return jnp.where(lane == 127, up_edge, up) + jnp.where(lane == 0, down_edge, down)


def stencil(source, source_row, kappa, kappa_row, rows):
    shape = (rows, SUB, 128)
    lane = lax.broadcasted_iota(jnp.int32, shape, 2)
    sub = lax.broadcasted_iota(jnp.int32, shape, 1)

    def part(ref, row):
        return ref[pl.ds(pl.multiple_of(row * SUB, SUB), rows * SUB), :].reshape(shape)

    center = part(source, source_row)
    around = part(source, source_row + 1) + part(source, source_row - 1)
    return (part(kappa, kappa_row) + 4.0) * center - around - lat_pair(center, lane, sub)


def kernel(
    dims, interp, value, weight, targets, count, kappa, out_solution, out_residual,
    blocks, values, weights, kappa_in, kap, grams, hot,
    codes, gather_one, gather_two, gather_three,
    right, inverse, z_own, z_ext, k_ext, y_own, w_own, w_ext, q_own,
    picks, sums, wide, plane_stats, column_stats,
    load_sem, orbit_send, orbit_recv, halo_send, halo_recv,
    plane_send, plane_recv, column_send, column_recv,
):
    orbits, ys, zs = dims
    slots = weights.shape[0]
    obs = weights.shape[2]
    rows = kappa_in.shape[0]
    tiles = rows * SUB
    plane = orbits * ys
    lons = ys * zs
    orbit = lax.axis_index("orbit")
    lon = lax.axis_index("lon")
    y = lon // zs
    z = lax.rem(lon, zs)
    east = lax.rem(lon + 1, lons)
    west = lax.rem(lon + lons - 1, lons)
    me_plane = orbit * ys + y

    per_chunk = slots // CHUNKS
    load_w = pltpu.make_async_copy(weight, weights, load_sem.at[0])
    load_v = pltpu.make_async_copy(value, values, load_sem.at[1])
    load_k = pltpu.make_async_copy(kappa, kappa_in, load_sem.at[2])
    load_w.start()
    load_v.start()
    loads = []
    for chunk in range(CHUNKS):
        part = pl.ds(chunk * per_chunk, per_chunk)
        loads.append(pltpu.make_async_copy(interp.at[part], blocks.at[part], load_sem.at[3 + chunk]))
        loads[-1].start()
    load_k.start()

    barrier = pltpu.get_barrier_semaphore()

    def plane_peer(step):
        there = lax.rem(me_plane + step, plane)
        return (there // ys, lax.rem(there, ys) * zs + z)

    def column_peer(step):
        return (orbit, y * zs + lax.rem(z + step, zs))

    @pl.loop(1, plane)
    def _(step):
        pl.semaphore_signal(barrier, inc=1, device_id=plane_peer(step), device_id_type=MESH)

    @pl.loop(1, zs)
    def _(step):
        pl.semaphore_signal(barrier, inc=1, device_id=column_peer(step), device_id_type=MESH)

    for side in (east, west):
        pl.semaphore_signal(barrier, inc=1, device_id=(orbit, side), device_id_type=MESH)

    lane_row = lax.broadcasted_iota(jnp.int32, (1, 128), 1)
    first_lane = lax.rem(orbit, 128 // slots) * slots
    live = count[0]
    code = jnp.zeros((1, 128), jnp.int32)
    for slot in range(slots):
        code = jnp.where(lane_row == first_lane + slot, targets[slot] + 1, code)
    code = jnp.where(lane_row - first_lane < live, code, 0)
    codes[orbit] = code.astype(F32)

    load_w.wait()
    load_v.wait()
    eye = lax.broadcasted_iota(jnp.int32, (128, 128), 0) == lax.broadcasted_iota(jnp.int32, (128, 128), 1)
    for chunk in range(CHUNKS):
        loads[chunk].wait()

        @pl.loop(chunk * per_chunk, (chunk + 1) * per_chunk)
        def _(slot):
            block = blocks[slot]
            weight_row = weights[slot]
            data = (weight_row * values[slot]).astype(BF16)
            high, low = split(block.T.astype(F32) * weight_row)
            left = jnp.concatenate([high, low, jnp.broadcast_to(data, (16, obs))], axis=0)
            product = jnp.dot(left, block, preferred_element_type=F32)
            factor = jnp.where(slot < live, 1.0, 0.0)
            gram = (product[:128] + product[128:256]) * factor
            grams[slot] = gram
            gather_one[orbit, pl.ds(slot, 1), :] = product[256:257] * factor
            gather_one[orbit, pl.ds(slots + slot, 1), :] = jnp.sum(
                jnp.where(eye, gram, 0.0), axis=0, keepdims=True
            )

    load_k.wait()

    @pl.loop(0, rows // SUB)
    def _(group):
        for tile in range(SUB):
            kap[pl.ds((group * SUB + 1) * SUB + tile, SUB, stride=SUB), :] = kappa_in[
                pl.ds(pl.multiple_of(group * SUB, SUB), SUB), tile * 128 : (tile + 1) * 128
            ]

    pl.semaphore_wait(barrier, (plane - 1) + (zs - 1) + 2)

    def orbit_copy(buffer, which, step):
        return pltpu.make_async_remote_copy(
            src_ref=buffer.at[orbit],
            dst_ref=buffer.at[orbit],
            send_sem=orbit_send.at[which, step],
            recv_sem=orbit_recv.at[which, step],
            device_id=(lax.rem(orbit + step, orbits), lon),
            device_id_type=MESH,
        )

    def orbit_start(buffer, which):
        for step in range(1, orbits):
            orbit_copy(buffer, which, step).start()

    def orbit_wait(buffer, which):
        for step in range(1, orbits):
            orbit_copy(buffer, which, step).wait_recv()

    def halo_copy(source, source_row, target, target_row, count_rows, which, side, device):
        return pltpu.make_async_remote_copy(
            src_ref=source.at[pl.ds(source_row * SUB, count_rows * SUB)],
            dst_ref=target.at[pl.ds(target_row * SUB, count_rows * SUB)],
            send_sem=halo_send.at[which, side],
            recv_sem=halo_recv.at[which, side],
            device_id=(orbit, device),
            device_id_type=MESH,
        )

    orbit_start(codes, 0)
    orbit_start(gather_one, 1)
    kap_halo = [
        halo_copy(kap, rows, kap, 0, 1, 0, 0, east),
        halo_copy(kap, 1, kap, rows + 1, 1, 0, 1, west),
    ]
    for copy in kap_halo:
        copy.start()

    orbit_wait(codes, 0)
    groups = hot.shape[1] // 128
    per_group = orbits // groups
    for group in range(groups):
        row = codes[group * per_group]
        for member in range(1, per_group):
            row = row + codes[group * per_group + member]
        part = 64

        @pl.loop(0, tiles // part)
        def _(step):
            offset = pl.multiple_of(step * part, part)
            cell = lax.broadcasted_iota(jnp.int32, (part, 128), 0) + (offset + 1)
            hot[pl.ds(offset, part), group * 128 : (group + 1) * 128] = jnp.where(
                cell.astype(F32) == row, 1.0, 0.0
            ).astype(BF16)

    def scatter(terms):
        high, low = split(terms)
        wide[...] = jnp.dot(hot[...], jnp.concatenate([high, low], axis=1), preferred_element_type=F32)

    def slot_rows(buffer, first):
        return buffer[:, first : first + slots, :].reshape(orbits * slots, 128)

    piece = 8 * SUB

    def each_piece(body):
        @pl.loop(0, tiles // piece)
        def _(step):
            body(pl.multiple_of(step * piece, piece))

    def added(offset):
        both = wide[pl.ds(offset, piece), :]
        return both[:, :128] + both[:, 128:]

    orbit_wait(gather_one, 1)
    scatter(slot_rows(gather_one, slots))

    def make_inverse(offset):
        shifted = kap[pl.ds(offset + SUB, piece), :] + 4.0
        inverse[pl.ds(offset, piece), :] = 1.0 / (prior_weight * (shifted * shifted + 4.0) + added(offset))

    each_piece(make_inverse)
    scatter(slot_rows(gather_one, 0))

    def make_z(offset):
        data = added(offset)
        right[pl.ds(offset, piece), :] = data
        scaled = data * inverse[pl.ds(offset, piece), :]
        z_own[pl.ds(offset, piece), :] = scaled
        z_ext[pl.ds(offset + 2 * SUB, piece), :] = scaled

    each_piece(make_z)

    def field_halo(own, ext, which):
        return [
            halo_copy(own, rows - 2, ext, 0, 2, which, 0, east),
            halo_copy(own, 0, ext, rows + 2, 2, which, 1, west),
        ]

    z_halo = field_halo(z_own, z_ext, 1)
    for copy in z_halo:
        copy.start()

    def apply_grams(own, gather):
        for slot in range(slots):
            picks[slot : slot + 1, :] = own[pl.ds(targets[slot], 1), :]
        columns = picks[...].T
        for slot in range(slots):
            column = jnp.broadcast_to(columns[:, slot : slot + 1], (128, 128))
            sums[slot * SUB : (slot + 1) * SUB, :] = jnp.sum(
                (grams[slot] * column).reshape(128 // SUB, SUB, 128), axis=0
            )
        total = sums[pl.ds(0, slots, stride=SUB), :]
        for part in range(1, SUB):
            total = total + sums[pl.ds(part, slots, stride=SUB), :]
        gather[orbit] = total
        return total

    apply_grams(z_own, gather_two)
    orbit_start(gather_two, 2)

    for copy in kap_halo:
        copy.wait_recv()
    for copy in z_halo:
        copy.wait_recv()

    first_rows = 6

    def first_stencil(ext):
        @pl.loop(0, (rows + 2) // first_rows)
        def _(step):
            row = step * first_rows
            k_ext[pl.ds(pl.multiple_of(row * SUB, SUB), first_rows * SUB), :] = stencil(
                ext, row + 1, kap, row, first_rows
            ).reshape(first_rows * SUB, 128)

    def second_stencil(target):
        @pl.loop(0, rows // SUB)
        def _(step):
            row = step * SUB
            target[pl.ds(pl.multiple_of(row * SUB, SUB), SUB * SUB), :] = prior_weight * stencil(
                k_ext, row + 1, kap, row + 1, SUB
            ).reshape(SUB * SUB, 128)

    first_stencil(z_ext)
    second_stencil(y_own)

    orbit_wait(gather_two, 2)
    scatter(slot_rows(gather_two, 0))

    def make_w(offset):
        part = pl.ds(offset, piece)
        image = y_own[part, :] + added(offset)
        y_own[part, :] = image
        scaled = image * inverse[part, :]
        w_own[part, :] = scaled
        w_ext[pl.ds(offset + 2 * SUB, piece), :] = scaled

    each_piece(make_w)
    w_halo = field_halo(w_own, w_ext, 2)
    for copy in w_halo:
        copy.start()

    terms = apply_grams(w_own, gather_three)
    orbit_start(gather_three, 3)
    last = jnp.sum((picks[...][:slots] * terms).reshape(slots // SUB, SUB, 128), axis=0)

    share_rows = rows // orbits
    share_row = orbit * share_rows
    share = pl.ds(pl.multiple_of(share_row * SUB, SUB), share_rows * SUB)

    def folded(product):
        return jnp.sum(product.reshape(share_rows, SUB, 128), axis=0)

    products = [
        folded(right[share, :] * z_own[share, :]),
        folded(y_own[share, :] * z_own[share, :]),
        folded(y_own[share, :] * w_own[share, :]),
    ]
    for copy in w_halo:
        copy.wait_recv()
    own_k = stencil(w_ext, share_row + 2, kap, share_row + 1, share_rows)
    products.append(last + prior_weight * jnp.sum(own_k * own_k, axis=0))
    row_index = lax.broadcasted_iota(jnp.int32, (SUB, 128), 0)
    lane_index = lax.broadcasted_iota(jnp.int32, (SUB, 128), 1)
    stacked = jnp.zeros((SUB, 128), F32)
    for index, product in enumerate(products):
        stacked = jnp.where(row_index == index, jnp.sum(product, axis=0, keepdims=True), stacked)
    stacked = stacked + pltpu.roll(stacked, 64, axis=1)
    stacked = stacked + pltpu.roll(stacked, 32, axis=1)
    packed = jnp.sum(jnp.where(lane_index // 32 == row_index, stacked, 0.0), axis=0, keepdims=True)
    plane_stats[me_plane] = packed

    def plane_copy(step):
        return pltpu.make_async_remote_copy(
            src_ref=plane_stats.at[me_plane],
            dst_ref=plane_stats.at[me_plane],
            send_sem=plane_send.at[step],
            recv_sem=plane_recv.at[step],
            device_id=plane_peer(step),
            device_id_type=MESH,
        )

    def column_copy(step):
        return pltpu.make_async_remote_copy(
            src_ref=column_stats.at[z],
            dst_ref=column_stats.at[z],
            send_sem=column_send.at[step],
            recv_sem=column_recv.at[step],
            device_id=column_peer(step),
            device_id_type=MESH,
        )

    @pl.loop(1, plane)
    def _(step):
        plane_copy(step).start()

    first_stencil(w_ext)

    @pl.loop(1, plane)
    def _(step):
        plane_copy(step).wait_recv()

    total = plane_stats[0]
    for index in range(1, plane):
        total = total + plane_stats[index]
    column_stats[z] = total

    @pl.loop(1, zs)
    def _(step):
        column_copy(step).start()

    second_stencil(q_own)
    orbit_wait(gather_three, 3)
    scatter(slot_rows(gather_three, 0))

    def make_q(offset):
        part = pl.ds(offset, piece)
        q_own[part, :] = q_own[part, :] + added(offset)

    each_piece(make_q)

    @pl.loop(1, zs)
    def _(step):
        column_copy(step).wait_recv()

    total = column_stats[0]
    for index in range(1, zs):
        total = total + column_stats[index]
    g = [
        jnp.sum(jnp.where(lane_row // 32 == index, total, 0.0), axis=1, keepdims=True)
        for index in range(4)
    ]
    alpha = g[0] / g[1]
    later = alpha * alpha * g[2] - g[0]
    grow = 1.0 + later / g[0]
    alpha_later = later / (grow * grow * g[1] - 2.0 * grow * alpha * g[2] + alpha * alpha * g[3])
    on_first = alpha + alpha_later * grow
    on_second = alpha_later * alpha

    def finish(offset):
        part = pl.ds(offset, piece)
        w_own[part, :] = on_first * z_own[part, :] - on_second * w_own[part, :]
        q_own[part, :] = right[part, :] - on_first * y_own[part, :] + on_second * q_own[part, :]

    for copy in w_halo:
        copy.wait_send()
    each_piece(finish)

    @pl.loop(0, rows // SUB)
    def _(group):
        for tile in range(SUB):
            strided = pl.ds(group * SUB * SUB + tile, SUB, stride=SUB)
            place = pl.ds(pl.multiple_of(group * SUB, SUB), SUB)
            out_solution[place, tile * 128 : (tile + 1) * 128] = w_own[strided, :]
            out_residual[place, tile * 128 : (tile + 1) * 128] = q_own[strided, :]

    for which, buffer in enumerate((codes, gather_one, gather_two, gather_three)):
        for step in range(1, orbits):
            orbit_copy(buffer, which, step).wait_send()
    for copy in kap_halo + z_halo:
        copy.wait_send()

    @pl.loop(1, plane)
    def _(step):
        plane_copy(step).wait_send()

    @pl.loop(1, zs)
    def _(step):
        column_copy(step).wait_send()


def solution(mesh):
    return build(mesh, 4, 16)


def build(mesh, ys, zs):
    orbits = mesh.shape["orbit"]

    def per_device(interp, obs_value, obs_weight, block_map, live_count, kappa2):
        slots, _, obs, cells = interp.shape
        rows, lat = kappa2.shape
        tiles = rows * lat // cells
        plane = orbits * ys
        hot_width = max(orbits * slots, 128)
        vmem = pltpu.VMEM
        field = vmem((tiles, 128), F32)
        extended = vmem((tiles + 4 * SUB, 128), F32)
        inner = vmem((tiles + 2 * SUB, 128), F32)
        gather = vmem((orbits, slots, 128), F32)
        return pl.pallas_call(
            functools.partial(kernel, (orbits, ys, zs)),
            out_shape=(
                jax.ShapeDtypeStruct(kappa2.shape, F32),
                jax.ShapeDtypeStruct(kappa2.shape, F32),
            ),
            in_specs=[
                pl.BlockSpec(memory_space=pl.ANY),
                pl.BlockSpec(memory_space=pl.ANY),
                pl.BlockSpec(memory_space=pl.ANY),
                pl.BlockSpec(memory_space=pltpu.SMEM),
                pl.BlockSpec(memory_space=pltpu.SMEM),
                pl.BlockSpec(memory_space=pl.ANY),
            ],
            out_specs=(pl.BlockSpec(memory_space=vmem), pl.BlockSpec(memory_space=vmem)),
            scratch_shapes=[
                vmem((slots, obs, cells), BF16),
                vmem((slots, 1, obs), F32),
                vmem((slots, 1, obs), F32),
                vmem((rows, lat), F32),
                inner,
                vmem((slots, 128, 128), F32),
                vmem((tiles, hot_width), BF16),
                vmem((orbits, 1, 128), F32),
                vmem((orbits, 2 * slots, 128), F32),
                gather,
                gather,
                field,
                field,
                field,
                extended,
                inner,
                field,
                field,
                extended,
                field,
                vmem((slots, 128), F32),
                vmem((slots * SUB, 128), F32),
                vmem((tiles, 256), F32),
                vmem((plane, 1, 128), F32),
                vmem((zs, 1, 128), F32),
                pltpu.SemaphoreType.DMA((3 + CHUNKS,)),
                pltpu.SemaphoreType.DMA((4, orbits)),
                pltpu.SemaphoreType.DMA((4, orbits)),
                pltpu.SemaphoreType.DMA((3, 2)),
                pltpu.SemaphoreType.DMA((3, 2)),
                pltpu.SemaphoreType.DMA((plane,)),
                pltpu.SemaphoreType.DMA((plane,)),
                pltpu.SemaphoreType.DMA((zs,)),
                pltpu.SemaphoreType.DMA((zs,)),
            ],
            compiler_params=pltpu.CompilerParams(
                collective_id=0, has_side_effects=True, vmem_limit_bytes=48 * 1024 * 1024
            ),
        )(
            interp.reshape(slots, obs, cells),
            obs_value,
            obs_weight,
            block_map.reshape(slots),
            live_count.reshape(1),
            kappa2,
        )

    in_specs = (
        P("orbit", "lon", None, None),
        P("orbit", "lon", None),
        P("orbit", "lon", None),
        P("orbit", "lon"),
        P("orbit", "lon"),
        P("lon", None),
    )
    out_specs = (P("lon", None), P("lon", None))
    return jax.shard_map(
        per_device, mesh=mesh, in_specs=in_specs, out_specs=out_specs, check_vma=False
    )
```

time: 711 us -> 57.4 us (0.08)
  the two profiles are of different devices: /device:TPU:2 before, /device:TPU:1 now
where the time goes in v1:
time: 57.4 us; the launch traced here: 57 us
  Pallas kernels  49.6 us (86%)
  local copies, waits for them, and re-layouts  6.11 us (11%)
  between operations  1.3 us (2%)
    pallas_call x1, Pallas kernels, per_device(): pl.pallas_call(functools.partial(kernel, (orbits, ys, zs)), out_shape=(ja...  49.6 us
    unnamed x12, local copies, waits for them, and re-layouts  6.11 us

profile of v1, /device:TPU:1, one launch (start us, length us, event | category | flops | bytes accessed | tf_op | source)
XLA Modules:
  0.0 57.0 jit_solution(5528959522212541122)
XLA Ops:
  1.3 0.0 copy-start
  1.3 1.6 %copy-done = bf16[32,1,256,128]{3,2,1,0:T(8,128)(2,1)S(1)} copy-done((bf16[32,1,256,128]{3,2,1,0:T(8,128)(2,1)S(1)}, bf16[32,1,256,128]{3,2,1,0:T(8,128)(2,1)}, u32[]{:S(2)}) %copy-start) | copy-done | bytes 2097176
  2.9 0.0 copy-start.1
  2.9 0.9 %copy-done.1 = f32[64,1024]{1,0:T(8,128)S(1)} copy-done((f32[64,1024]{1,0:T(8,128)S(1)}, f32[64,1024]{1,0:T(8,128)}, u32[]{:S(2)}) %copy-start.1) | copy-done | bytes 262168
  3.8 0.0 copy-start.2
  3.8 0.8 %copy-done.2 = f32[32,1,256]{2,1,0:T(1,128)S(1)} copy-done((f32[32,1,256]{2,1,0:T(1,128)S(1)}, f32[32,1,256]{2,1,0:T(1,128)}, u32[]{:S(2)}) %copy-start.2) | copy-done | bytes 32792
  4.6 0.0 copy-start.3
  4.6 0.8 %copy-done.3 = f32[32,1,256]{2,1,0:T(1,128)S(1)} copy-done((f32[32,1,256]{2,1,0:T(1,128)S(1)}, f32[32,1,256]{2,1,0:T(1,128)}, u32[]{:S(2)}) %copy-start.3) | copy-done | bytes 32792
  5.3 0.0 copy-start.4
  5.3 0.7 %copy-done.4 = s32[32,1]{0,1:T(1,128)S(1)} copy-done((s32[32,1]{0,1:T(1,128)S(1)}, s32[32,1]{0,1:T(1,128)}, u32[]{:S(2)}) %copy-start.4) | copy-done | bytes 152
  6.0 49.6 %shard_map.77 = (f32[64,1024]{1,0:T(8,128)S(1)}, f32[64,1024]{1,0:T(8,128)S(1)}) custom-call(bf16[32,256,128]{2,1,0:T(8,128)(2,1)S(1)} %bitcast.4, f32[32,1,256]{2,1,0:T(1,128)S(1)} %copy-done.2, f32[32,1,256]{2,1,0:T(1,128)S(1)} %copy-done.3, s32[32]{0:T(128)S(1)} %bitcast.5, s32[1]{0:T(128)} %bitcast.3.count, f32[64,1024]{1,0:T(8,128)S(1)} %copy-done.1), custom_call_target="tpu_custom_call" | custom-call | tf_op jit(solution)/shard_map/pallas_call | solution.py:452
  55.6 0.7 %copy.11 = f32[64,1024]{1,0:T(8,128)} copy(f32[64,1024]{1,0:T(8,128)S(1)} %get-tuple-element.4) | data formatting | bytes 524288
  56.3 0.7 %copy.12 = f32[64,1024]{1,0:T(8,128)} copy(f32[64,1024]{1,0:T(8,128)S(1)} %get-tuple-element.5) | data formatting | bytes 524288
Async XLA Ops:
  1.3 1.6 %copy-start = (bf16[32,1,256,128]{3,2,1,0:T(8,128)(2,1)S(1)}, bf16[32,1,256,128]{3,2,1,0:T(8,128)(2,1)}, u32[]{:S(2)}) copy-start(bf16[32,1,256,128]{3,2,1,0:T(8,128)(2,1)} %param.6) | copy-start | bytes 6291460
  2.9 0.9 %copy-start.1 = (f32[64,1024]{1,0:T(8,128)S(1)}, f32[64,1024]{1,0:T(8,128)}, u32[]{:S(2)}) copy-start(f32[64,1024]{1,0:T(8,128)} %kappa.1) | copy-start | bytes 786436
  3.8 0.8 %copy-start.2 = (f32[32,1,256]{2,1,0:T(1,128)S(1)}, f32[32,1,256]{2,1,0:T(1,128)}, u32[]{:S(2)}) copy-start(f32[32,1,256]{2,1,0:T(1,128)} %value.1) | copy-start | bytes 98308
  4.6 0.8 %copy-start.3 = (f32[32,1,256]{2,1,0:T(1,128)S(1)}, f32[32,1,256]{2,1,0:T(1,128)}, u32[]{:S(2)}) copy-start(f32[32,1,256]{2,1,0:T(1,128)} %weight.1) | copy-start | bytes 98308
  5.3 0.7 %copy-start.4 = (s32[32,1]{0,1:T(1,128)S(1)}, s32[32,1]{0,1:T(1,128)}, u32[]{:S(2)}) copy-start(s32[32,1]{0,1:T(1,128)} %param.9) | copy-start | bytes 388

commit v2 on v1

--- a/solution.py
+++ b/solution.py
@@ -14,6 +14,8 @@
 prior_weight = 0.0625
 SUB = 8
 CHUNKS = 4
+SPLIT = (12, 24)
+SPLIT_OF = 32
 
 
 def split(value):
@@ -43,15 +45,16 @@
 
 
 def kernel(
-    dims, interp, value, weight, targets, count, kappa, out_solution, out_residual,
-    blocks, values, weights, kappa_in, kap, grams, hot,
+    dims, interp, value, weight, targets_hbm, count_hbm, kappa, out_solution, out_residual,
+    targets, count, blocks, values, weights, kappa_in, kap_own, kap, grams, hot, match,
     codes, gather_one, gather_two, gather_three,
-    right, inverse, z_own, z_ext, k_ext, y_own, w_own, w_ext, q_own,
-    picks, sums, wide, plane_stats, column_stats,
-    load_sem, orbit_send, orbit_recv, halo_send, halo_recv,
-    plane_send, plane_recv, column_send, column_recv,
+    right, inverse, z_own, z_ext, k_ext, y_own, w_own, w_edge, w_ext, q_own,
+    kap_picks, inverse_picks, picks, sums, wide, plane_stats, column_stats,
+    load_sem, orbit_send, orbit_recv, one_send, one_recv, halo_send, halo_recv,
+    plane_send, plane_recv, column_send, column_recv, known,
 ):
     orbits, ys, zs = dims
+    xs = orbits // 2
     slots = weights.shape[0]
     obs = weights.shape[2]
     rows = kappa_in.shape[0]
@@ -60,6 +63,8 @@
     lons = ys * zs
     orbit = lax.axis_index("orbit")
     lon = lax.axis_index("lon")
+    x = orbit // 2
+    core = lax.rem(orbit, 2)
     y = lon // zs
     z = lax.rem(lon, zs)
     east = lax.rem(lon + 1, lons)
@@ -67,6 +72,8 @@
     me_plane = orbit * ys + y
 
     per_chunk = slots // CHUNKS
+    load_t = pltpu.make_async_copy(targets_hbm, targets, load_sem.at[3 + CHUNKS])
+    load_c = pltpu.make_async_copy(count_hbm, count, load_sem.at[4 + CHUNKS])
     load_w = pltpu.make_async_copy(weight, weights, load_sem.at[0])
     load_v = pltpu.make_async_copy(value, values, load_sem.at[1])
     load_k = pltpu.make_async_copy(kappa, kappa_in, load_sem.at[2])
@@ -77,9 +84,9 @@
         part = pl.ds(chunk * per_chunk, per_chunk)
         loads.append(pltpu.make_async_copy(interp.at[part], blocks.at[part], load_sem.at[3 + chunk]))
         loads[-1].start()
+    load_t.start()
+    load_c.start()
     load_k.start()
-
-    barrier = pltpu.get_barrier_semaphore()
 
     def plane_peer(step):
         there = lax.rem(me_plane + step, plane)
@@ -88,58 +95,54 @@
     def column_peer(step):
         return (orbit, y * zs + lax.rem(z + step, zs))
 
-    @pl.loop(1, plane)
-    def _(step):
-        pl.semaphore_signal(barrier, inc=1, device_id=plane_peer(step), device_id_type=MESH)
-
-    @pl.loop(1, zs)
-    def _(step):
-        pl.semaphore_signal(barrier, inc=1, device_id=column_peer(step), device_id_type=MESH)
-
-    for side in (east, west):
-        pl.semaphore_signal(barrier, inc=1, device_id=(orbit, side), device_id_type=MESH)
-
+    def signal(semaphore, device):
+        pl.semaphore_signal(semaphore, inc=1, device_id=device, device_id_type=MESH)
+
+    def both_ways(step):
+        return sorted({step % zs, -step % zs} - {0})
+
+    def learned(which, step):
+        if both_ways(step):
+            pl.semaphore_wait(known.at[which], len(both_ways(step)))
+
+    barrier = pltpu.get_barrier_semaphore()
+    near = [(lax.rem(orbit + step, orbits), lon) for step in range(1, orbits)]
+    near += [(orbit, lax.rem(y + step, ys) * zs + z) for step in range(1, ys)]
+    near += [column_peer(step) for step in sorted({1 % zs, -1 % zs, 2 % zs, -2 % zs} - {0})]
+    near += [(orbit, east), (orbit, west)]
+    for device in near:
+        signal(barrier, device)
+
+    load_w.wait()
+    load_v.wait()
+    load_c.wait()
+    live = count[0, 0]
+    first_row = lax.broadcasted_iota(jnp.int32, (16, obs), 0) == 0
+    for chunk in range(CHUNKS):
+        loads[chunk].wait()
+
+        @pl.loop(chunk * per_chunk, (chunk + 1) * per_chunk, unroll=2)
+        def _(slot):
+            block = blocks[slot]
+            weight_row = weights[slot]
+            left = jnp.where(first_row, weight_row * values[slot], weight_row).astype(BF16)
+            product = jnp.dot(
+                left, jnp.concatenate([block, block * block], axis=1), preferred_element_type=F32
+            )
+            factor = jnp.where(slot < live, 1.0, 0.0)
+            gather_one[orbit, pl.ds(slot, 1), :] = product[0:1, :128] * factor
+            gather_one[orbit, pl.ds(slots + slot, 1), :] = product[1:2, 128:] * factor
+
+    load_t.wait()
     lane_row = lax.broadcasted_iota(jnp.int32, (1, 128), 1)
     first_lane = lax.rem(orbit, 128 // slots) * slots
-    live = count[0]
     code = jnp.zeros((1, 128), jnp.int32)
     for slot in range(slots):
         code = jnp.where(lane_row == first_lane + slot, targets[slot] + 1, code)
     code = jnp.where(lane_row - first_lane < live, code, 0)
     codes[orbit] = code.astype(F32)
 
-    load_w.wait()
-    load_v.wait()
-    eye = lax.broadcasted_iota(jnp.int32, (128, 128), 0) == lax.broadcasted_iota(jnp.int32, (128, 128), 1)
-    for chunk in range(CHUNKS):
-        loads[chunk].wait()
-
-        @pl.loop(chunk * per_chunk, (chunk + 1) * per_chunk)
-        def _(slot):
-            block = blocks[slot]
-            weight_row = weights[slot]
-            data = (weight_row * values[slot]).astype(BF16)
-            high, low = split(block.T.astype(F32) * weight_row)
-            left = jnp.concatenate([high, low, jnp.broadcast_to(data, (16, obs))], axis=0)
-            product = jnp.dot(left, block, preferred_element_type=F32)
-            factor = jnp.where(slot < live, 1.0, 0.0)
-            gram = (product[:128] + product[128:256]) * factor
-            grams[slot] = gram
-            gather_one[orbit, pl.ds(slot, 1), :] = product[256:257] * factor
-            gather_one[orbit, pl.ds(slots + slot, 1), :] = jnp.sum(
-                jnp.where(eye, gram, 0.0), axis=0, keepdims=True
-            )
-
-    load_k.wait()
-
-    @pl.loop(0, rows // SUB)
-    def _(group):
-        for tile in range(SUB):
-            kap[pl.ds((group * SUB + 1) * SUB + tile, SUB, stride=SUB), :] = kappa_in[
-                pl.ds(pl.multiple_of(group * SUB, SUB), SUB), tile * 128 : (tile + 1) * 128
-            ]
-
-    pl.semaphore_wait(barrier, (plane - 1) + (zs - 1) + 2)
+    pl.semaphore_wait(barrier, len(near))
 
     def orbit_copy(buffer, which, step):
         return pltpu.make_async_remote_copy(
@@ -159,6 +162,29 @@
         for step in range(1, orbits):
             orbit_copy(buffer, which, step).wait_recv()
 
+    def one_copy(owner, device, index):
+        return pltpu.make_async_remote_copy(
+            src_ref=gather_one.at[owner],
+            dst_ref=gather_one.at[owner],
+            send_sem=one_send.at[index],
+            recv_sem=one_recv.at[index],
+            device_id=(device, lon),
+            device_id_type=MESH,
+        )
+
+    def along(step):
+        return lax.rem(x + step + xs, xs) * 2 + core
+
+    partner = x * 2 + 1 - core
+    x_steps = sorted(range(1, xs), key=lambda step: min(step, xs - step))
+    own_copies = [one_copy(orbit, along(step), step) for step in reversed(x_steps)]
+    own_copies.append(one_copy(orbit, partner, 0))
+    for copy in own_copies:
+        copy.start()
+    orbit_start(codes, 0)
+    for step in both_ways(2):
+        signal(known.at[0], column_peer(step))
+
     def halo_copy(source, source_row, target, target_row, count_rows, which, side, device):
         return pltpu.make_async_remote_copy(
             src_ref=source.at[pl.ds(source_row * SUB, count_rows * SUB)],
@@ -169,14 +195,47 @@
             device_id_type=MESH,
         )
 
-    orbit_start(codes, 0)
-    orbit_start(gather_one, 1)
+    load_k.wait()
+
+    @pl.loop(0, rows // SUB)
+    def _(group):
+        for tile in range(SUB):
+            values_here = kappa_in[
+                pl.ds(pl.multiple_of(group * SUB, SUB), SUB), tile * 128 : (tile + 1) * 128
+            ]
+            kap[pl.ds((group * SUB + 1) * SUB + tile, SUB, stride=SUB), :] = values_here
+            kap_own[pl.ds(group * SUB * SUB + tile, SUB, stride=SUB), :] = values_here
+
     kap_halo = [
-        halo_copy(kap, rows, kap, 0, 1, 0, 0, east),
-        halo_copy(kap, 1, kap, rows + 1, 1, 0, 1, west),
+        halo_copy(kap_own, rows - 1, kap, 0, 1, 0, 0, east),
+        halo_copy(kap_own, 0, kap, rows + 1, 1, 0, 1, west),
     ]
     for copy in kap_halo:
         copy.start()
+
+    def pick(own, target):
+        for slot in range(slots):
+            target[slot : slot + 1, :] = own[pl.ds(targets[slot], 1), :]
+
+    pick(kap_own, kap_picks)
+
+    def make_grams(begin, end):
+        @pl.loop(begin, end)
+        def _(slot):
+            block = blocks[slot]
+            high, low = split(block.T.astype(F32) * weights[slot])
+            product = jnp.dot(jnp.concatenate([high, low], axis=0), block, preferred_element_type=F32)
+            grams[slot] = (product[:128] + product[128:]) * jnp.where(slot < live, 1.0, 0.0)
+
+    forwards = []
+
+    def forward(step):
+        one_copy(orbit, along(step), step).wait_recv()
+        forwards.append(one_copy(along(-step), partner, xs - 1 + step))
+        forwards[-1].start()
+
+    cuts = [0] + [slots * part // SPLIT_OF for part in SPLIT] + [slots]
+    make_grams(cuts[0], cuts[1])
 
     orbit_wait(codes, 0)
     groups = hot.shape[1] // 128
@@ -186,18 +245,32 @@
         for member in range(1, per_group):
             row = row + codes[group * per_group + member]
         part = 64
+        columns = slice(group * 128, (group + 1) * 128)
+        for slot in range(slots):
+            wanted = (targets[slot] + 1).astype(F32)
+            match[slot : slot + 1, columns] = jnp.where(row == wanted, 1.0, 0.0)
 
         @pl.loop(0, tiles // part)
         def _(step):
             offset = pl.multiple_of(step * part, part)
             cell = lax.broadcasted_iota(jnp.int32, (part, 128), 0) + (offset + 1)
-            hot[pl.ds(offset, part), group * 128 : (group + 1) * 128] = jnp.where(
-                cell.astype(F32) == row, 1.0, 0.0
-            ).astype(BF16)
+            hot[pl.ds(offset, part), columns] = jnp.where(cell.astype(F32) == row, 1.0, 0.0).astype(BF16)
+
+    for step in x_steps[:2]:
+        forward(step)
+    make_grams(cuts[1], cuts[2])
+    for step in x_steps[2:]:
+        forward(step)
+    make_grams(cuts[2], cuts[3])
+
+    def halves(terms):
+        return jnp.concatenate(split(terms), axis=1)
+
+    def joined(product):
+        return product[:, :128] + product[:, 128:]
 
     def scatter(terms):
-        high, low = split(terms)
-        wide[...] = jnp.dot(hot[...], jnp.concatenate([high, low], axis=1), preferred_element_type=F32)
+        wide[...] = jnp.dot(hot[...], halves(terms), preferred_element_type=F32)
 
     def slot_rows(buffer, first):
         return buffer[:, first : first + slots, :].reshape(orbits * slots, 128)
@@ -210,42 +283,10 @@
             body(pl.multiple_of(step * piece, piece))
 
     def added(offset):
-        both = wide[pl.ds(offset, piece), :]
-        return both[:, :128] + both[:, 128:]
-
-    orbit_wait(gather_one, 1)
-    scatter(slot_rows(gather_one, slots))
-
-    def make_inverse(offset):
-        shifted = kap[pl.ds(offset + SUB, piece), :] + 4.0
-        inverse[pl.ds(offset, piece), :] = 1.0 / (prior_weight * (shifted * shifted + 4.0) + added(offset))
-
-    each_piece(make_inverse)
-    scatter(slot_rows(gather_one, 0))
-
-    def make_z(offset):
-        data = added(offset)
-        right[pl.ds(offset, piece), :] = data
-        scaled = data * inverse[pl.ds(offset, piece), :]
-        z_own[pl.ds(offset, piece), :] = scaled
-        z_ext[pl.ds(offset + 2 * SUB, piece), :] = scaled
-
-    each_piece(make_z)
-
-    def field_halo(own, ext, which):
-        return [
-            halo_copy(own, rows - 2, ext, 0, 2, which, 0, east),
-            halo_copy(own, 0, ext, rows + 2, 2, which, 1, west),
-        ]
-
-    z_halo = field_halo(z_own, z_ext, 1)
-    for copy in z_halo:
-        copy.start()
-
-    def apply_grams(own, gather):
-        for slot in range(slots):
-            picks[slot : slot + 1, :] = own[pl.ds(targets[slot], 1), :]
-        columns = picks[...].T
+        return joined(wide[pl.ds(offset, piece), :])
+
+    def apply_grams(picked, gather):
+        columns = picked.T
         for slot in range(slots):
             column = jnp.broadcast_to(columns[:, slot : slot + 1], (128, 128))
             sums[slot * SUB : (slot + 1) * SUB, :] = jnp.sum(
@@ -257,12 +298,49 @@
         gather[orbit] = total
         return total
 
-    apply_grams(z_own, gather_two)
+    one_copy(orbit, partner, 0).wait_recv()
+    for step in x_steps:
+        one_copy(orbit, partner, xs - 1 + step).wait_recv()
+    learned(0, 2)
+    for step in both_ways(4):
+        signal(known.at[1], column_peer(step))
+
+    matches = match[...].astype(BF16)
+    diagonal = slot_rows(gather_one, slots)
+    data = slot_rows(gather_one, 0)
+    shifted = kap_picks[...] + 4.0
+    diagonal_here = joined(jnp.dot(matches, halves(diagonal), preferred_element_type=F32))
+    data_here = joined(jnp.dot(matches, halves(data), preferred_element_type=F32))
+    inverse_here = 1.0 / (prior_weight * (shifted * shifted + 4.0) + diagonal_here)
+    inverse_picks[...] = inverse_here
+    apply_grams(data_here * inverse_here, gather_two)
     orbit_start(gather_two, 2)
 
-    for copy in kap_halo:
-        copy.wait_recv()
+    scatter(diagonal)
+
+    def make_inverse(offset):
+        shifted = kap_own[pl.ds(offset, piece), :] + 4.0
+        inverse[pl.ds(offset, piece), :] = 1.0 / (prior_weight * (shifted * shifted + 4.0) + added(offset))
+
+    each_piece(make_inverse)
+    scatter(data)
+
+    def make_z(offset):
+        data_part = added(offset)
+        right[pl.ds(offset, piece), :] = data_part
+        scaled = data_part * inverse[pl.ds(offset, piece), :]
+        z_own[pl.ds(offset, piece), :] = scaled
+        z_ext[pl.ds(offset + 2 * SUB, piece), :] = scaled
+
+    each_piece(make_z)
+
+    z_halo = [
+        halo_copy(z_own, rows - 2, z_ext, 0, 2, 1, 0, east),
+        halo_copy(z_own, 0, z_ext, rows + 2, 2, 1, 1, west),
+    ]
     for copy in z_halo:
+        copy.start()
+    for copy in kap_halo + z_halo:
         copy.wait_recv()
 
     first_rows = 6
@@ -285,9 +363,26 @@
 
     first_stencil(z_ext)
     second_stencil(y_own)
+    pick(y_own, picks)
 
     orbit_wait(gather_two, 2)
-    scatter(slot_rows(gather_two, 0))
+    terms = slot_rows(gather_two, 0)
+    edge = 2 * SUB
+    tail = tiles - edge
+    ahead = jnp.concatenate([hot[0:edge], hot[tail:tiles], matches], axis=0)
+    early = joined(jnp.dot(ahead, halves(terms), preferred_element_type=F32))
+    w_edge[0:edge] = (y_own[0:edge] + early[0:edge]) * inverse[0:edge]
+    w_edge[edge : 2 * edge] = (y_own[tail:tiles] + early[edge : 2 * edge]) * inverse[tail:tiles]
+    w_halo = [
+        halo_copy(w_edge, 2, w_ext, 0, 2, 2, 0, east),
+        halo_copy(w_edge, 0, w_ext, rows + 2, 2, 2, 1, west),
+    ]
+    for copy in w_halo:
+        copy.start()
+    w_here = (picks[...] + early[2 * edge :]) * inverse_picks[...]
+    w_terms = apply_grams(w_here, gather_three)
+    last = jnp.sum((w_here * w_terms).reshape(slots // SUB, SUB, 128), axis=0)
+    scatter(terms)
 
     def make_w(offset):
         part = pl.ds(offset, piece)
@@ -298,13 +393,6 @@
         w_ext[pl.ds(offset + 2 * SUB, piece), :] = scaled
 
     each_piece(make_w)
-    w_halo = field_halo(w_own, w_ext, 2)
-    for copy in w_halo:
-        copy.start()
-
-    terms = apply_grams(w_own, gather_three)
-    orbit_start(gather_three, 3)
-    last = jnp.sum((picks[...][:slots] * terms).reshape(slots // SUB, SUB, 128), axis=0)
 
     share_rows = rows // orbits
     share_row = orbit * share_rows
@@ -356,6 +444,7 @@
     def _(step):
         plane_copy(step).start()
 
+    orbit_start(gather_three, 3)
     first_stencil(w_ext)
 
     @pl.loop(1, plane)
@@ -366,6 +455,7 @@
     for index in range(1, plane):
         total = total + plane_stats[index]
     column_stats[z] = total
+    learned(1, 4)
 
     @pl.loop(1, zs)
     def _(step):
@@ -404,8 +494,6 @@
         w_own[part, :] = on_first * z_own[part, :] - on_second * w_own[part, :]
         q_own[part, :] = right[part, :] - on_first * y_own[part, :] + on_second * q_own[part, :]
 
-    for copy in w_halo:
-        copy.wait_send()
     each_piece(finish)
 
     @pl.loop(0, rows // SUB)
@@ -416,10 +504,10 @@
             out_solution[place, tile * 128 : (tile + 1) * 128] = w_own[strided, :]
             out_residual[place, tile * 128 : (tile + 1) * 128] = q_own[strided, :]
 
-    for which, buffer in enumerate((codes, gather_one, gather_two, gather_three)):
+    for which, buffer in ((0, codes), (2, gather_two), (3, gather_three)):
         for step in range(1, orbits):
             orbit_copy(buffer, which, step).wait_send()
-    for copy in kap_halo + z_halo:
+    for copy in own_copies + forwards + kap_halo + z_halo + w_halo:
         copy.wait_send()
 
     @pl.loop(1, plane)
@@ -452,26 +540,23 @@
         return pl.pallas_call(
             functools.partial(kernel, (orbits, ys, zs)),
             out_shape=(
-                jax.ShapeDtypeStruct(kappa2.shape, F32),
-                jax.ShapeDtypeStruct(kappa2.shape, F32),
+                pltpu.VMEM(kappa2.shape, F32),
+                pltpu.VMEM(kappa2.shape, F32),
             ),
-            in_specs=[
-                pl.BlockSpec(memory_space=pl.ANY),
-                pl.BlockSpec(memory_space=pl.ANY),
-                pl.BlockSpec(memory_space=pl.ANY),
-                pl.BlockSpec(memory_space=pltpu.SMEM),
-                pl.BlockSpec(memory_space=pltpu.SMEM),
-                pl.BlockSpec(memory_space=pl.ANY),
-            ],
+            in_specs=[pl.BlockSpec(memory_space=pltpu.HBM)] * 6,
             out_specs=(pl.BlockSpec(memory_space=vmem), pl.BlockSpec(memory_space=vmem)),
             scratch_shapes=[
+                pltpu.SMEM((slots,), jnp.int32),
+                pltpu.SMEM((1, 1), jnp.int32),
                 vmem((slots, obs, cells), BF16),
                 vmem((slots, 1, obs), F32),
                 vmem((slots, 1, obs), F32),
                 vmem((rows, lat), F32),
+                field,
                 inner,
                 vmem((slots, 128, 128), F32),
                 vmem((tiles, hot_width), BF16),
+                vmem((slots, hot_width), F32),
                 vmem((orbits, 1, 128), F32),
                 vmem((orbits, 2 * slots, 128), F32),
                 gather,
@@ -483,32 +568,38 @@
                 inner,
                 field,
                 field,
+                vmem((4 * SUB, 128), F32),
                 extended,
                 field,
+                vmem((slots, 128), F32),
+                vmem((slots, 128), F32),
                 vmem((slots, 128), F32),
                 vmem((slots * SUB, 128), F32),
                 vmem((tiles, 256), F32),
                 vmem((plane, 1, 128), F32),
                 vmem((zs, 1, 128), F32),
-                pltpu.SemaphoreType.DMA((3 + CHUNKS,)),
+                pltpu.SemaphoreType.DMA((5 + CHUNKS,)),
                 pltpu.SemaphoreType.DMA((4, orbits)),
                 pltpu.SemaphoreType.DMA((4, orbits)),
+                pltpu.SemaphoreType.DMA((orbits,)),
+                pltpu.SemaphoreType.DMA((orbits,)),
                 pltpu.SemaphoreType.DMA((3, 2)),
                 pltpu.SemaphoreType.DMA((3, 2)),
                 pltpu.SemaphoreType.DMA((plane,)),
                 pltpu.SemaphoreType.DMA((plane,)),
                 pltpu.SemaphoreType.DMA((zs,)),
                 pltpu.SemaphoreType.DMA((zs,)),
+                pltpu.SemaphoreType.REGULAR((2,)),
             ],
             compiler_params=pltpu.CompilerParams(
-                collective_id=0, has_side_effects=True, vmem_limit_bytes=48 * 1024 * 1024
+                collective_id=0, has_side_effects=True, vmem_limit_bytes=66400000
             ),
         )(
             interp.reshape(slots, obs, cells),
             obs_value,
             obs_weight,
             block_map.reshape(slots),
-            live_count.reshape(1),
+            live_count,
             kappa2,
         )
 

time: 57.4 us -> 51.2 us (0.89)
  local copies, waits for them, and re-layouts: 6.11 us -> 1.41 us
  Pallas kernels: 49.6 us -> 48.4 us
    unnamed x12 -> x2, local copies, waits for them, and re-layouts: 6.11 us -> 1.41 us
    pallas_call x1, Pallas kernels: 49.6 us -> 48.4 us  [per_device(): pl.pallas_call(functools.partial(kernel, (orbits, ys, zs)), out_shape=(pl...]
where the time goes in v2:
time: 51.2 us; the launch traced here: 51.1 us
  Pallas kernels  48.4 us (95%)
  local copies, waits for them, and re-layouts  1.41 us (3%)
  between operations  1.29 us (3%)
    pallas_call x1, Pallas kernels, per_device(): pl.pallas_call(functools.partial(kernel, (orbits, ys, zs)), out_shape=(pl...  48.4 us
    unnamed x2, local copies, waits for them, and re-layouts  1.41 us

profile of v2, /device:TPU:1, one launch (start us, length us, event | category | flops | bytes accessed | tf_op | source)
XLA Modules:
  0.0 51.1 jit_solution(3015018341135192219)
XLA Ops:
  1.3 48.4 %shard_map.77 = (f32[64,1024]{1,0:T(8,128)S(1)}, f32[64,1024]{1,0:T(8,128)S(1)}) custom-call(bf16[32,256,128]{2,1,0:T(8,128)(2,1)} %bitcast.2, f32[32,1,256]{2,1,0:T(1,128)} %value.1, f32[32,1,256]{2,1,0:T(1,128)} %weight.1, s32[32]{0:T(128)} %bitcast.3, s32[1,1]{1,0:T(1,128)S(6)} %copy.12.count_hbm, f32[64,1024]{1,0:T(8,128)} %kappa.1), custom_call_target="tpu_custom_call" | custom-call | tf_op jit(solution)/shard_map/pallas_call | solution.py:540
  49.7 0.7 %copy.10 = f32[64,1024]{1,0:T(8,128)} copy(f32[64,1024]{1,0:T(8,128)S(1)} %get-tuple-element.2) | data formatting | bytes 524288
  50.4 0.7 %copy.11 = f32[64,1024]{1,0:T(8,128)} copy(f32[64,1024]{1,0:T(8,128)S(1)} %get-tuple-element.3) | data formatting | bytes 524288

commit v3 on v2

--- a/solution.py
+++ b/solution.py
@@ -23,6 +23,12 @@
     return high, (value - high.astype(F32)).astype(BF16)
 
 
+def tree_sum(values):
+    while len(values) > 1:
+        values = [sum(values[at : at + 2][1:], values[at]) for at in range(0, len(values), 2)]
+    return values[0]
+
+
 def lat_pair(cells, lane, sub):
     up = pltpu.roll(cells, 127, axis=2)
     down = pltpu.roll(cells, 1, axis=2)
@@ -45,11 +51,11 @@
 
 
 def kernel(
-    dims, interp, value, weight, targets_hbm, count_hbm, kappa, out_solution, out_residual,
+    dims, interp, value, weight, targets_hbm, count_hbm, kappa, out_z, out_w, out_right, out_y, out_q, out_first, out_second,
     targets, count, blocks, values, weights, kappa_in, kap_own, kap, grams, hot, match,
     codes, gather_one, gather_two, gather_three,
-    right, inverse, z_own, z_ext, k_ext, y_own, w_own, w_edge, w_ext, q_own,
-    kap_picks, inverse_picks, picks, sums, wide, plane_stats, column_stats,
+    right, inverse, z_own, z_edge, z_ext, k_ext, y_own, w_own, w_edge, w_ext, q_own,
+    kap_picks, inverse_picks, picks, wide, plane_stats, column_stats,
     load_sem, orbit_send, orbit_recv, one_send, one_recv, halo_send, halo_recv,
     plane_send, plane_recv, column_send, column_recv, known,
 ):
@@ -121,7 +127,7 @@
     for chunk in range(CHUNKS):
         loads[chunk].wait()
 
-        @pl.loop(chunk * per_chunk, (chunk + 1) * per_chunk, unroll=2)
+        @pl.loop(chunk * per_chunk, (chunk + 1) * per_chunk, unroll=per_chunk)
         def _(slot):
             block = blocks[slot]
             weight_row = weights[slot]
@@ -197,7 +203,7 @@
 
     load_k.wait()
 
-    @pl.loop(0, rows // SUB)
+    @pl.loop(0, rows // SUB, unroll=2)
     def _(group):
         for tile in range(SUB):
             values_here = kappa_in[
@@ -219,13 +225,19 @@
 
     pick(kap_own, kap_picks)
 
+    def halves(terms):
+        return jnp.concatenate(split(terms), axis=1)
+
+    def joined(product):
+        return product[:, :128] + product[:, 128:]
+
     def make_grams(begin, end):
-        @pl.loop(begin, end)
+        @pl.loop(begin, end, unroll=4)
         def _(slot):
             block = blocks[slot]
-            high, low = split(block.T.astype(F32) * weights[slot])
-            product = jnp.dot(jnp.concatenate([high, low], axis=0), block, preferred_element_type=F32)
-            grams[slot] = (product[:128] + product[128:]) * jnp.where(slot < live, 1.0, 0.0)
+            left = (block.T.astype(F32) * weights[slot]).astype(BF16)
+            product = jnp.dot(left, block, preferred_element_type=F32)
+            grams[slot] = halves(product * jnp.where(slot < live, 1.0, 0.0))
 
     forwards = []
 
@@ -250,7 +262,7 @@
             wanted = (targets[slot] + 1).astype(F32)
             match[slot : slot + 1, columns] = jnp.where(row == wanted, 1.0, 0.0)
 
-        @pl.loop(0, tiles // part)
+        @pl.loop(0, tiles // part, unroll=4)
         def _(step):
             offset = pl.multiple_of(step * part, part)
             cell = lax.broadcasted_iota(jnp.int32, (part, 128), 0) + (offset + 1)
@@ -263,12 +275,6 @@
         forward(step)
     make_grams(cuts[2], cuts[3])
 
-    def halves(terms):
-        return jnp.concatenate(split(terms), axis=1)
-
-    def joined(product):
-        return product[:, :128] + product[:, 128:]
-
     def scatter(terms):
         wide[...] = jnp.dot(hot[...], halves(terms), preferred_element_type=F32)
 
@@ -278,23 +284,37 @@
     piece = 8 * SUB
 
     def each_piece(body):
-        @pl.loop(0, tiles // piece)
+        @pl.loop(0, tiles // piece, unroll=4)
         def _(step):
             body(pl.multiple_of(step * piece, piece))
 
     def added(offset):
         return joined(wide[pl.ds(offset, piece), :])
 
+    sub_index = lax.broadcasted_iota(jnp.int32, (SUB, 128), 0)
+    even = lax.rem(sub_index, 2) == 0
+
     def apply_grams(picked, gather):
-        columns = picked.T
-        for slot in range(slots):
-            column = jnp.broadcast_to(columns[:, slot : slot + 1], (128, 128))
-            sums[slot * SUB : (slot + 1) * SUB, :] = jnp.sum(
-                (grams[slot] * column).reshape(128 // SUB, SUB, 128), axis=0
-            )
-        total = sums[pl.ds(0, slots, stride=SUB), :]
-        for part in range(1, SUB):
-            total = total + sums[pl.ds(part, slots, stride=SUB), :]
+        results = []
+        for first in range(0, slots, SUB):
+            rows_here = picked[first : first + SUB]
+            high = rows_here.astype(BF16).astype(F32)
+            stack = jnp.concatenate([high, rows_here - high], axis=0)
+            both = jnp.concatenate([even, even], axis=0)
+            left = jnp.concatenate(
+                [jnp.where(both, stack, 0.0), jnp.where(both, 0.0, stack)], axis=1
+            ).astype(BF16)
+            result = None
+            for pair in range(SUB // 2):
+                slot = first + 2 * pair
+                product = jnp.dot(
+                    left, grams[slot : slot + 2].reshape(256, 256), preferred_element_type=F32
+                )
+                product = joined(product)
+                product = product[:SUB] + product[SUB:]
+                result = product if result is None else jnp.where(sub_index // 2 == pair, product, result)
+            results.append(result)
+        total = jnp.concatenate(results, axis=0)
         gather[orbit] = total
         return total
 
@@ -305,22 +325,38 @@
     for step in both_ways(4):
         signal(known.at[1], column_peer(step))
 
-    matches = match[...].astype(BF16)
+    edge = 2 * SUB
+    tail = tiles - edge
+    ahead = jnp.concatenate([hot[0:edge], hot[tail:tiles], match[...].astype(BF16)], axis=0)
+
+    def early(terms):
+        return joined(jnp.dot(ahead, halves(terms), preferred_element_type=F32))
+
+    def inverse_of(kappa_part, diagonal_part):
+        shifted = kappa_part + 4.0
+        return 1.0 / (prior_weight * (shifted * shifted + 4.0) + diagonal_part)
+
     diagonal = slot_rows(gather_one, slots)
     data = slot_rows(gather_one, 0)
-    shifted = kap_picks[...] + 4.0
-    diagonal_here = joined(jnp.dot(matches, halves(diagonal), preferred_element_type=F32))
-    data_here = joined(jnp.dot(matches, halves(data), preferred_element_type=F32))
-    inverse_here = 1.0 / (prior_weight * (shifted * shifted + 4.0) + diagonal_here)
-    inverse_picks[...] = inverse_here
-    apply_grams(data_here * inverse_here, gather_two)
+    kap_ahead = jnp.concatenate([kap_own[0:edge], kap_own[tail:tiles], kap_picks[...]], axis=0)
+    inverse_ahead = inverse_of(kap_ahead, early(diagonal))
+    z_ahead = early(data) * inverse_ahead
+    z_edge[...] = z_ahead[: 2 * edge]
+    z_halo = [
+        halo_copy(z_edge, 2, z_ext, 0, 2, 1, 0, east),
+        halo_copy(z_edge, 0, z_ext, rows + 2, 2, 1, 1, west),
+    ]
+    for copy in z_halo:
+        copy.start()
+    inverse_picks[...] = inverse_ahead[2 * edge :]
+    apply_grams(z_ahead[2 * edge :], gather_two)
     orbit_start(gather_two, 2)
 
     scatter(diagonal)
 
     def make_inverse(offset):
-        shifted = kap_own[pl.ds(offset, piece), :] + 4.0
-        inverse[pl.ds(offset, piece), :] = 1.0 / (prior_weight * (shifted * shifted + 4.0) + added(offset))
+        part = pl.ds(offset, piece)
+        inverse[part, :] = inverse_of(kap_own[part, :], added(offset))
 
     each_piece(make_inverse)
     scatter(data)
@@ -334,19 +370,13 @@
 
     each_piece(make_z)
 
-    z_halo = [
-        halo_copy(z_own, rows - 2, z_ext, 0, 2, 1, 0, east),
-        halo_copy(z_own, 0, z_ext, rows + 2, 2, 1, 1, west),
-    ]
-    for copy in z_halo:
-        copy.start()
     for copy in kap_halo + z_halo:
         copy.wait_recv()
 
-    first_rows = 6
+    first_rows = 11
 
     def first_stencil(ext):
-        @pl.loop(0, (rows + 2) // first_rows)
+        @pl.loop(0, (rows + 2) // first_rows, unroll=2)
         def _(step):
             row = step * first_rows
             k_ext[pl.ds(pl.multiple_of(row * SUB, SUB), first_rows * SUB), :] = stencil(
@@ -354,7 +384,7 @@
             ).reshape(first_rows * SUB, 128)
 
     def second_stencil(target):
-        @pl.loop(0, rows // SUB)
+        @pl.loop(0, rows // SUB, unroll=2)
         def _(step):
             row = step * SUB
             target[pl.ds(pl.multiple_of(row * SUB, SUB), SUB * SUB), :] = prior_weight * stencil(
@@ -367,19 +397,18 @@
 
     orbit_wait(gather_two, 2)
     terms = slot_rows(gather_two, 0)
-    edge = 2 * SUB
-    tail = tiles - edge
-    ahead = jnp.concatenate([hot[0:edge], hot[tail:tiles], matches], axis=0)
-    early = joined(jnp.dot(ahead, halves(terms), preferred_element_type=F32))
-    w_edge[0:edge] = (y_own[0:edge] + early[0:edge]) * inverse[0:edge]
-    w_edge[edge : 2 * edge] = (y_own[tail:tiles] + early[edge : 2 * edge]) * inverse[tail:tiles]
+    terms_ahead = early(terms)
+    y_ahead = jnp.concatenate([y_own[0:edge], y_own[tail:tiles], picks[...]], axis=0)
+    inverse_ahead = jnp.concatenate([inverse[0:edge], inverse[tail:tiles], inverse_picks[...]], axis=0)
+    w_ahead = (y_ahead + terms_ahead) * inverse_ahead
+    w_edge[...] = w_ahead[: 2 * edge]
     w_halo = [
         halo_copy(w_edge, 2, w_ext, 0, 2, 2, 0, east),
         halo_copy(w_edge, 0, w_ext, rows + 2, 2, 2, 1, west),
     ]
     for copy in w_halo:
         copy.start()
-    w_here = (picks[...] + early[2 * edge :]) * inverse_picks[...]
+    w_here = w_ahead[2 * edge :]
     w_terms = apply_grams(w_here, gather_three)
     last = jnp.sum((w_here * w_terms).reshape(slots // SUB, SUB, 128), axis=0)
     scatter(terms)
@@ -410,14 +439,13 @@
         copy.wait_recv()
     own_k = stencil(w_ext, share_row + 2, kap, share_row + 1, share_rows)
     products.append(last + prior_weight * jnp.sum(own_k * own_k, axis=0))
-    row_index = lax.broadcasted_iota(jnp.int32, (SUB, 128), 0)
     lane_index = lax.broadcasted_iota(jnp.int32, (SUB, 128), 1)
     stacked = jnp.zeros((SUB, 128), F32)
     for index, product in enumerate(products):
-        stacked = jnp.where(row_index == index, jnp.sum(product, axis=0, keepdims=True), stacked)
+        stacked = jnp.where(sub_index == index, jnp.sum(product, axis=0, keepdims=True), stacked)
     stacked = stacked + pltpu.roll(stacked, 64, axis=1)
     stacked = stacked + pltpu.roll(stacked, 32, axis=1)
-    packed = jnp.sum(jnp.where(lane_index // 32 == row_index, stacked, 0.0), axis=0, keepdims=True)
+    packed = jnp.sum(jnp.where(lane_index // 32 == sub_index, stacked, 0.0), axis=0, keepdims=True)
     plane_stats[me_plane] = packed
 
     def plane_copy(step):
@@ -440,25 +468,35 @@
             device_id_type=MESH,
         )
 
-    @pl.loop(1, plane)
-    def _(step):
+    for step in range(1, plane):
         plane_copy(step).start()
 
     orbit_start(gather_three, 3)
+
+    def lay_out(source, target):
+        @pl.loop(0, rows // SUB, unroll=2)
+        def _(group):
+            for tile in range(SUB):
+                place = pl.ds(pl.multiple_of(group * SUB, SUB), SUB)
+                target[place, tile * 128 : (tile + 1) * 128] = source[
+                    pl.ds(group * SUB * SUB + tile, SUB, stride=SUB), :
+                ]
+
     first_stencil(w_ext)
+    lay_out(z_own, out_z)
+    lay_out(right, out_right)
+    lay_out(y_own, out_y)
+    lay_out(w_own, out_w)
 
     @pl.loop(1, plane)
     def _(step):
         plane_copy(step).wait_recv()
 
-    total = plane_stats[0]
-    for index in range(1, plane):
-        total = total + plane_stats[index]
+    total = tree_sum([plane_stats[index] for index in range(plane)])
     column_stats[z] = total
     learned(1, 4)
 
-    @pl.loop(1, zs)
-    def _(step):
+    for step in range(1, zs):
         column_copy(step).start()
 
     second_stencil(q_own)
@@ -470,14 +508,27 @@
         q_own[part, :] = q_own[part, :] + added(offset)
 
     each_piece(make_q)
+    lay_out(q_own, out_q)
+
+    for which, buffer in ((0, codes), (2, gather_two), (3, gather_three)):
+        for step in range(1, orbits):
+            orbit_copy(buffer, which, step).wait_send()
+    for copy in own_copies + forwards + kap_halo + z_halo + w_halo:
+        copy.wait_send()
+
+    @pl.loop(1, plane)
+    def _(step):
+        plane_copy(step).wait_send()
+
+    @pl.loop(1, zs)
+    def _(step):
+        column_copy(step).wait_send()
 
     @pl.loop(1, zs)
     def _(step):
         column_copy(step).wait_recv()
 
-    total = column_stats[0]
-    for index in range(1, zs):
-        total = total + column_stats[index]
+    total = tree_sum([column_stats[index] for index in range(zs)])
     g = [
         jnp.sum(jnp.where(lane_row // 32 == index, total, 0.0), axis=1, keepdims=True)
         for index in range(4)
@@ -489,34 +540,8 @@
     on_first = alpha + alpha_later * grow
     on_second = alpha_later * alpha
 
-    def finish(offset):
-        part = pl.ds(offset, piece)
-        w_own[part, :] = on_first * z_own[part, :] - on_second * w_own[part, :]
-        q_own[part, :] = right[part, :] - on_first * y_own[part, :] + on_second * q_own[part, :]
-
-    each_piece(finish)
-
-    @pl.loop(0, rows // SUB)
-    def _(group):
-        for tile in range(SUB):
-            strided = pl.ds(group * SUB * SUB + tile, SUB, stride=SUB)
-            place = pl.ds(pl.multiple_of(group * SUB, SUB), SUB)
-            out_solution[place, tile * 128 : (tile + 1) * 128] = w_own[strided, :]
-            out_residual[place, tile * 128 : (tile + 1) * 128] = q_own[strided, :]
-
-    for which, buffer in ((0, codes), (2, gather_two), (3, gather_three)):
-        for step in range(1, orbits):
-            orbit_copy(buffer, which, step).wait_send()
-    for copy in own_copies + forwards + kap_halo + z_halo + w_halo:
-        copy.wait_send()
-
-    @pl.loop(1, plane)
-    def _(step):
-        plane_copy(step).wait_send()
-
-    @pl.loop(1, zs)
-    def _(step):
-        column_copy(step).wait_send()
+    out_first[...] = on_first
+    out_second[...] = on_second
 
 
 def solution(mesh):
@@ -537,14 +562,14 @@
         extended = vmem((tiles + 4 * SUB, 128), F32)
         inner = vmem((tiles + 2 * SUB, 128), F32)
         gather = vmem((orbits, slots, 128), F32)
-        return pl.pallas_call(
+        z, w, right, y, q, on_first, on_second = pl.pallas_call(
             functools.partial(kernel, (orbits, ys, zs)),
             out_shape=(
-                pltpu.VMEM(kappa2.shape, F32),
-                pltpu.VMEM(kappa2.shape, F32),
+                *([pltpu.VMEM(kappa2.shape, F32)] * 5),
+                *([pltpu.VMEM((1, 1), F32)] * 2),
             ),
             in_specs=[pl.BlockSpec(memory_space=pltpu.HBM)] * 6,
-            out_specs=(pl.BlockSpec(memory_space=vmem), pl.BlockSpec(memory_space=vmem)),
+            out_specs=(pl.BlockSpec(memory_space=vmem),) * 7,
             scratch_shapes=[
                 pltpu.SMEM((slots,), jnp.int32),
                 pltpu.SMEM((1, 1), jnp.int32),
@@ -554,7 +579,7 @@
                 vmem((rows, lat), F32),
                 field,
                 inner,
-                vmem((slots, 128, 128), F32),
+                vmem((slots, 128, 256), BF16),
                 vmem((tiles, hot_width), BF16),
                 vmem((slots, hot_width), F32),
                 vmem((orbits, 1, 128), F32),
@@ -564,6 +589,7 @@
                 field,
                 field,
                 field,
+                vmem((4 * SUB, 128), F32),
                 extended,
                 inner,
                 field,
@@ -574,7 +600,6 @@
                 vmem((slots, 128), F32),
                 vmem((slots, 128), F32),
                 vmem((slots, 128), F32),
-                vmem((slots * SUB, 128), F32),
                 vmem((tiles, 256), F32),
                 vmem((plane, 1, 128), F32),
                 vmem((zs, 1, 128), F32),
@@ -592,7 +617,7 @@
                 pltpu.SemaphoreType.REGULAR((2,)),
             ],
             compiler_params=pltpu.CompilerParams(
-                collective_id=0, has_side_effects=True, vmem_limit_bytes=66400000
+                collective_id=0, has_side_effects=True, vmem_limit_bytes=65600000
             ),
         )(
             interp.reshape(slots, obs, cells),
@@ -602,6 +627,8 @@
             live_count,
             kappa2,
         )
+        on_first, on_second = on_first.reshape(()), on_second.reshape(())
+        return on_first * z - on_second * w, right - on_first * y + on_second * q
 
     in_specs = (
         P("orbit", "lon", None, None),

time: 51.2 us -> 45.9 us (0.90)
  Pallas kernels: 48.4 us -> 42.3 us
  other arithmetic: 0 us -> 2.16 us
  local copies, waits for them, and re-layouts: 1.41 us -> 0 us
    pallas_call x1, Pallas kernels: 48.4 us -> 42.3 us  [per_device(): pl.pallas_call(functools.partial(kernel, (orbits, ys, zs)), out_shape=(*[...]
    add x0 -> x1, other arithmetic: none -> 2.16 us  [per_device(): return (on_first * z - on_second * w, right - on_first * y + on_second * q)]
    unnamed x2 -> x0, local copies, waits for them, and re-layouts: 1.41 us -> none
where the time goes in v3:
time: 45.9 us; the launch traced here: 45.7 us
  Pallas kernels  42.3 us (92%)
  other arithmetic  2.16 us (5%)
  between operations  1.29 us (3%)
    pallas_call x1, Pallas kernels, per_device(): pl.pallas_call(functools.partial(kernel, (orbits, ys, zs)), out_shape=(*[...  42.3 us
    add x1, other arithmetic, per_device(): return (on_first * z - on_second * w, right - on_first * y + on_second * q)  2.16 us

profile of v3, /device:TPU:1, one launch (start us, length us, event | category | flops | bytes accessed | tf_op | source)
XLA Modules:
  0.0 45.7 jit_solution(4442405004526682907)
XLA Ops:
  1.3 42.3 %shard_map.77 = (f32[64,1024]{1,0:T(8,128)S(1)}, f32[64,1024]{1,0:T(8,128)S(1)}, f32[64,1024]{1,0:T(8,128)S(1)}, f32[64,1024]{1,0:T(8,128)S(1)}, f32[64,1024]{1,...) custom-call(bf16[32,256,128]{2,1,0:T(8,128)(2,1)} %bitcast.4, f32[32,1,256]{2,1,0:T(1,128)} %value.1, ...), custom_call_target="tpu_custom_call" | custom-call | tf_op jit(solution)/shard_map/pallas_call | solution.py:565
  43.6 2.2 %multiply_add_fusion = (f32[64,1024]{1,0:T(8,128)}, f32[64,1024]{1,0:T(8,128)}) fusion(f32[64,1024]{1,0:T(8,128)S(1)} %get-tuple-element.15, f32[64,1024]{1,0:T(8,128)S(1)} %get-tuple-element.13, f32[64,1024]{1,0:T(8,128)S(1)} %get-tuple-element.14, f32[]{:T(128)} %bitcast.3, f32[]{:T(128)} %bitcast.2, f32[64,1024]{1,0:T(8,128)S(1)} %get-tuple-element.12, ...), kind=kLoop, calls=%fused_computation | loop fusion | flops 458752 | bytes 1835016 | tf_op jit(solution)/shard_map/add | solution.py:631

commit v4 on v3

--- a/solution.py
+++ b/solution.py
@@ -14,7 +14,7 @@
 prior_weight = 0.0625
 SUB = 8
 CHUNKS = 4
-SPLIT = (12, 24)
+SPLIT = (16, 24)
 SPLIT_OF = 32
 
 
@@ -54,10 +54,10 @@
     dims, interp, value, weight, targets_hbm, count_hbm, kappa, out_z, out_w, out_right, out_y, out_q, out_first, out_second,
     targets, count, blocks, values, weights, kappa_in, kap_own, kap, grams, hot, match,
     codes, gather_one, gather_two, gather_three,
-    right, inverse, z_own, z_edge, z_ext, k_ext, y_own, w_own, w_edge, w_ext, q_own,
-    kap_picks, inverse_picks, picks, wide, plane_stats, column_stats,
+    right, inverse, z_own, z_edge, z_ext, k_ext, y_own, w_own, w_edge, w_land, w_ext, q_own,
+    kap_picks, inverse_picks, picks, wide, plane_stats, cross_stats, column_stats,
     load_sem, orbit_send, orbit_recv, one_send, one_recv, halo_send, halo_recv,
-    plane_send, plane_recv, column_send, column_recv, known,
+    plane_send, plane_recv, cross_send, cross_recv, column_send, column_recv, known,
 ):
     orbits, ys, zs = dims
     xs = orbits // 2
@@ -161,7 +161,7 @@
         )
 
     def orbit_start(buffer, which):
-        for step in range(1, orbits):
+        for step in sorted(range(1, orbits), key=lambda step: -min(step, orbits - step)):
             orbit_copy(buffer, which, step).start()
 
     def orbit_wait(buffer, which):
@@ -185,9 +185,9 @@
     x_steps = sorted(range(1, xs), key=lambda step: min(step, xs - step))
     own_copies = [one_copy(orbit, along(step), step) for step in reversed(x_steps)]
     own_copies.append(one_copy(orbit, partner, 0))
+    orbit_start(codes, 0)
     for copy in own_copies:
         copy.start()
-    orbit_start(codes, 0)
     for step in both_ways(2):
         signal(known.at[0], column_peer(step))
 
@@ -393,6 +393,8 @@
 
     first_stencil(z_ext)
     second_stencil(y_own)
+    w_ext[0:edge] = jnp.zeros((edge, 128), F32)
+    w_ext[tiles + edge : tiles + 2 * edge] = jnp.zeros((edge, 128), F32)
     pick(y_own, picks)
 
     orbit_wait(gather_two, 2)
@@ -403,8 +405,8 @@
     w_ahead = (y_ahead + terms_ahead) * inverse_ahead
     w_edge[...] = w_ahead[: 2 * edge]
     w_halo = [
-        halo_copy(w_edge, 2, w_ext, 0, 2, 2, 0, east),
-        halo_copy(w_edge, 0, w_ext, rows + 2, 2, 2, 1, west),
+        halo_copy(w_edge, 2, w_land, 0, 2, 2, 0, east),
+        halo_copy(w_edge, 0, w_land, 2, 2, 2, 1, west),
     ]
     for copy in w_halo:
         copy.start()
@@ -435,18 +437,21 @@
         folded(y_own[share, :] * z_own[share, :]),
         folded(y_own[share, :] * w_own[share, :]),
     ]
-    for copy in w_halo:
-        copy.wait_recv()
     own_k = stencil(w_ext, share_row + 2, kap, share_row + 1, share_rows)
-    products.append(last + prior_weight * jnp.sum(own_k * own_k, axis=0))
+    head_row, tail_row = w_own[0:SUB], w_own[tiles - SUB : tiles]
+    edges = (head_row * head_row + tail_row * tail_row) * (1.0 / orbits)
+    products.append(last + prior_weight * (jnp.sum(own_k * own_k, axis=0) + edges))
     lane_index = lax.broadcasted_iota(jnp.int32, (SUB, 128), 1)
     stacked = jnp.zeros((SUB, 128), F32)
     for index, product in enumerate(products):
         stacked = jnp.where(sub_index == index, jnp.sum(product, axis=0, keepdims=True), stacked)
-    stacked = stacked + pltpu.roll(stacked, 64, axis=1)
-    stacked = stacked + pltpu.roll(stacked, 32, axis=1)
-    packed = jnp.sum(jnp.where(lane_index // 32 == sub_index, stacked, 0.0), axis=0, keepdims=True)
-    plane_stats[me_plane] = packed
+
+    def folded_lanes(value):
+        value = value + pltpu.roll(value, 64, axis=1)
+        return value + pltpu.roll(value, 32, axis=1)
+
+    packed = jnp.where(lane_index // 32 == sub_index, folded_lanes(stacked), 0.0)
+    plane_stats[me_plane] = jnp.sum(packed, axis=0, keepdims=True)
 
     def plane_copy(step):
         return pltpu.make_async_remote_copy(
@@ -458,6 +463,16 @@
             device_id_type=MESH,
         )
 
+    def cross_copy(step):
+        return pltpu.make_async_remote_copy(
+            src_ref=cross_stats.at[y],
+            dst_ref=cross_stats.at[y],
+            send_sem=cross_send.at[step],
+            recv_sem=cross_recv.at[step],
+            device_id=(orbit, lax.rem(y + step, ys) * zs + z),
+            device_id_type=MESH,
+        )
+
     def column_copy(step):
         return pltpu.make_async_remote_copy(
             src_ref=column_stats.at[z],
@@ -471,6 +486,18 @@
     for step in range(1, plane):
         plane_copy(step).start()
 
+    first_k = stencil(w_ext, 2, kap, 1, 1)[0]
+    last_k = stencil(w_ext, rows + 1, kap, rows, 1)[0]
+    for copy in w_halo:
+        copy.wait_recv()
+    cross = first_k * w_land[SUB : 2 * SUB] + last_k * w_land[2 * SUB : 3 * SUB]
+    cross = folded_lanes(jnp.broadcast_to(jnp.sum(cross, axis=0, keepdims=True), (SUB, 128)))
+    cross_stats[y] = jnp.where(lane_row >= 96, (-2.0 * prior_weight) * cross[0:1], 0.0)
+    for step in range(1, ys):
+        cross_copy(step).start()
+    w_ext[0:edge] = w_land[0:edge]
+    w_ext[tiles + edge : tiles + 2 * edge] = w_land[edge : 2 * edge]
+
     orbit_start(gather_three, 3)
 
     def lay_out(source, target):
@@ -492,7 +519,10 @@
     def _(step):
         plane_copy(step).wait_recv()
 
+    for step in range(1, ys):
+        cross_copy(step).wait_recv()
     total = tree_sum([plane_stats[index] for index in range(plane)])
+    total = total + tree_sum([cross_stats[index] for index in range(ys)])
     column_stats[z] = total
     learned(1, 4)
 
@@ -515,6 +545,8 @@
             orbit_copy(buffer, which, step).wait_send()
     for copy in own_copies + forwards + kap_halo + z_halo + w_halo:
         copy.wait_send()
+    for step in range(1, ys):
+        cross_copy(step).wait_send()
 
     @pl.loop(1, plane)
     def _(step):
@@ -542,6 +574,29 @@
 
     out_first[...] = on_first
     out_second[...] = on_second
+
+
+PIECES = 4
+
+
+def combine(first, second, z, w, right, y, q, out_solution, out_residual, solution_piece, residual_piece, sem):
+    rows = z.shape[0] // PIECES
+    on_first, on_second = first[...], second[...]
+    copies = []
+    for piece in range(PIECES):
+        part = pl.ds(piece * rows, rows)
+        solution_piece[part, :] = on_first * z[part, :] - on_second * w[part, :]
+        copies.append(
+            pltpu.make_async_copy(solution_piece.at[part], out_solution.at[part], sem.at[0, piece])
+        )
+        copies[-1].start()
+        residual_piece[part, :] = right[part, :] - on_first * y[part, :] + on_second * q[part, :]
+        copies.append(
+            pltpu.make_async_copy(residual_piece.at[part], out_residual.at[part], sem.at[1, piece])
+        )
+        copies[-1].start()
+    for copy in copies:
+        copy.wait()
 
 
 def solution(mesh):
@@ -595,6 +650,7 @@
                 field,
                 field,
                 vmem((4 * SUB, 128), F32),
+                vmem((4 * SUB, 128), F32),
                 extended,
                 field,
                 vmem((slots, 128), F32),
@@ -602,6 +658,7 @@
                 vmem((slots, 128), F32),
                 vmem((tiles, 256), F32),
                 vmem((plane, 1, 128), F32),
+                vmem((ys, 1, 128), F32),
                 vmem((zs, 1, 128), F32),
                 pltpu.SemaphoreType.DMA((5 + CHUNKS,)),
                 pltpu.SemaphoreType.DMA((4, orbits)),
@@ -612,6 +669,8 @@
                 pltpu.SemaphoreType.DMA((3, 2)),
                 pltpu.SemaphoreType.DMA((plane,)),
                 pltpu.SemaphoreType.DMA((plane,)),
+                pltpu.SemaphoreType.DMA((ys,)),
+                pltpu.SemaphoreType.DMA((ys,)),
                 pltpu.SemaphoreType.DMA((zs,)),
                 pltpu.SemaphoreType.DMA((zs,)),
                 pltpu.SemaphoreType.REGULAR((2,)),
@@ -627,8 +686,18 @@
             live_count,
             kappa2,
         )
-        on_first, on_second = on_first.reshape(()), on_second.reshape(())
-        return on_first * z - on_second * w, right - on_first * y + on_second * q
+        return pl.pallas_call(
+            combine,
+            out_shape=(jax.ShapeDtypeStruct(kappa2.shape, F32),) * 2,
+            in_specs=[pl.BlockSpec(memory_space=vmem)] * 7,
+            out_specs=(pl.BlockSpec(memory_space=pltpu.HBM),) * 2,
+            scratch_shapes=[
+                vmem(kappa2.shape, F32),
+                vmem(kappa2.shape, F32),
+                pltpu.SemaphoreType.DMA((2, PIECES)),
+            ],
+            compiler_params=pltpu.CompilerParams(vmem_limit_bytes=4 * 1024 * 1024),
+        )(on_first, on_second, z, w, right, y, q)
 
     in_specs = (
         P("orbit", "lon", None, None),

time: 45.9 us -> 42.9 us (0.935)
  the two profiles are of different devices: /device:TPU:1 before, /device:TPU:2 now
where the time goes in v4:
time: 42.9 us; the launch traced here: 42.7 us
  Pallas kernels  41.4 us (97%)
  between operations  1.29 us (3%)
    pallas_call x1, Pallas kernels, per_device(): pl.pallas_call(functools.partial(kernel, (orbits, ys, zs)), out_shape=(*[...  39.3 us
    pallas_call x1, Pallas kernels, per_device(): pl.pallas_call(combine, out_shape=(jax.ShapeDtypeStruct(kappa2.shape, F32...  2.12 us

profile of v4, /device:TPU:2, one launch (start us, length us, event | category | flops | bytes accessed | tf_op | source)
XLA Modules:
  0.0 42.7 jit_solution(9763893995255468954)
XLA Ops:
  1.3 39.3 %shard_map.77 = (f32[64,1024]{1,0:T(8,128)S(1)}, f32[64,1024]{1,0:T(8,128)S(1)}, f32[64,1024]{1,0:T(8,128)S(1)}, f32[64,1024]{1,0:T(8,128)S(1)}, f32[64,1024]{1,...) custom-call(bf16[32,256,128]{2,1,0:T(8,128)(2,1)} %bitcast.2, f32[32,1,256]{2,1,0:T(1,128)} %value.1, ...), custom_call_target="tpu_custom_call" | custom-call | tf_op jit(solution)/shard_map/pallas_call | solution.py:620
  40.6 2.1 %shard_map.78 = (f32[64,1024]{1,0:T(8,128)}, f32[64,1024]{1,0:T(8,128)}) custom-call(f32[1,1]{1,0:T(1,128)} %get-tuple-element.9.first, f32[1,1]{1,0:T(1,128)} %get-tuple-element.10.second, f32[64,1024]{1,0:T(8,128)S(1)} %get-tuple-element.11.z, f32[64,1024]{1,0:T(8,128)S(1)} %get-tuple-element.12.w, f32[64,1024]{1,0:T(8,128)S(1)} %get-tuple-element.13.right, ...), custom_call_target="tpu_custom_call" | custom-call | tf_op jit(solution)/shard_map/pallas_call | solution.py:689
